TPU v7x, 32 devices: a whole 2x2x4 slice. The times are simulated.
32 devices in a mesh: subj: 4 (over y, x), slab: 8 (over z, core).
Axes of the slice: x: 2, y: 2, z: 4, core: 2. Of those that a mesh axis runs over, the one named last changes fastest.
Arguments:
- source_bricks: bfloat16 [4, 64, 48000], P('subj', 'slab'), may hold values from -6 to 6
- brick_ids: int32 [4, 256], P('subj', 'slab'), may hold values from 0 to 63, as said below
- brick_offsets: int32 [4, 3, 256], P('subj', None, 'slab'), may hold values from 0 to 4
- deformation: float32 [4, 3, 32, 64, 128], P('subj', None, 'slab'), may hold values from -0.3 to 0.3
Outputs:
- atlas_mean: float32 [6, 32, 64, 128], P(None, 'slab', 'subj')
Inputs may be any that keep to these rules, and one draw needn't show every extreme that they name: `brick_ids`: brick ids of slab k are k * 8 to (k + 1) * 8 - 1. Among the 32 template pieces of one slab and one subject, at most 6 source bricks lie in any one slab, and in every such list some slab is named exactly 6 times.
All inputs are finite; a program needn't handle non-finite values.
Results may differ from a plain program's by a relative error of at most 0.00095.
Values may be sent and summed in bfloat16 or wider, within the bound.
A program may use at most 128 MiB of HBM per device.

v0:
```python
import jax
import jax.numpy as jnp
from jax import lax
from jax.sharding import PartitionSpec as P

COMP = 6
BRICK = 16
PAD = 2
ZQ = 4
NEWTON = 2
SLAB_Z = 4


def extended(cells, sides, width):
    for axis, dim in sides:
        count = lax.axis_size(axis)
        ends = count - 1
        head = lax.slice_in_dim(cells, 0, width, axis=dim)
        tail = lax.slice_in_dim(cells, cells.shape[dim] - width, cells.shape[dim], axis=dim)
        cells = jnp.concatenate(
            [
                lax.ppermute(tail, axis, [(i, (i + 1) % count) for i in range(ends)]),
                cells,
                lax.ppermute(head, axis, [((i + 1) % count, i) for i in range(ends)]),
            ],
            axis=dim,
        )
    return cells


def crop_window(flat_brick, start_z, start_y, start_x):
    edge_full = BRICK + 2 * PAD
    brick_cube = flat_brick.reshape(COMP, edge_full, edge_full, edge_full)
    anchor = jnp.zeros((), jnp.int32)
    window = lax.dynamic_slice(
        brick_cube, (anchor, start_z, start_y, start_x), (COMP, SLAB_Z, BRICK, BRICK)
    )
    return window.reshape(COMP * SLAB_Z * BRICK * BRICK)


def jacobian(rimmed):
    along_z = (rimmed[:, 2:, 1:-1, 1:-1] - rimmed[:, :-2, 1:-1, 1:-1]) * 0.5
    along_y = (rimmed[:, 1:-1, 2:, 1:-1] - rimmed[:, 1:-1, :-2, 1:-1]) * 0.5
    along_x = (rimmed[:, 1:-1, 1:-1, 2:] - rimmed[:, 1:-1, 1:-1, :-2]) * 0.5
    gradients = (along_z, along_y, along_x)
    return [
        [gradients[col_at][row_at] + (1.0 if row_at == col_at else 0.0) for col_at in range(3)]
        for row_at in range(3)
    ]


def polar_factor(matrix):
    for newton_step in range(NEWTON):
        cofactor = [
            [
                matrix[(row_at + 1) % 3][(col_at + 1) % 3]
                * matrix[(row_at + 2) % 3][(col_at + 2) % 3]
                - matrix[(row_at + 1) % 3][(col_at + 2) % 3]
                * matrix[(row_at + 2) % 3][(col_at + 1) % 3]
                for col_at in range(3)
            ]
            for row_at in range(3)
        ]
        determinant = (
            matrix[0][0] * cofactor[0][0]
            + matrix[0][1] * cofactor[0][1]
            + matrix[0][2] * cofactor[0][2]
        )
        scaling = 1.0 / determinant
        matrix = [
            [
                0.5 * (matrix[row_at][col_at] + cofactor[row_at][col_at] * scaling)
                for col_at in range(3)
            ]
            for row_at in range(3)
        ]
    return matrix


def reorient(components, rotation):
    tensor_rows = [
        [components[0], components[3], components[4]],
        [components[3], components[1], components[5]],
        [components[4], components[5], components[2]],
    ]
    left_side = [
        [
            rotation[row_at][0] * tensor_rows[0][col_at]
            + rotation[row_at][1] * tensor_rows[1][col_at]
            + rotation[row_at][2] * tensor_rows[2][col_at]
            for col_at in range(3)
        ]
        for row_at in range(3)
    ]
    pair_list = ((0, 0), (1, 1), (2, 2), (0, 1), (0, 2), (1, 2))
    return [
        left_side[row_at][0] * rotation[col_at][0]
        + left_side[row_at][1] * rotation[col_at][1]
        + left_side[row_at][2] * rotation[col_at][2]
        for row_at, col_at in pair_list
    ]


def shards(source_bricks, brick_ids, brick_offsets, deformation):
    slab_count = lax.axis_size("slab")
    pieces_here = brick_ids.shape[1]
    held_count = source_bricks.shape[1]
    capacity = max(2, 3 * pieces_here // (2 * slab_count))
    slot_count = slab_count * capacity
    wanted_ids = brick_ids[0]
    owner_slab = wanted_ids // held_count
    local_index = wanted_ids % held_count
    positions = jnp.arange(pieces_here, dtype=jnp.int32)
    earlier = (owner_slab[:, None] == owner_slab[None, :]) & (
        positions[None, :] < positions[:, None]
    )
    ranking = jnp.sum(earlier.astype(jnp.int32), axis=1)
    slot_of = owner_slab * capacity + ranking
    slot_hits = (slot_of[:, None] == jnp.arange(slot_count, dtype=jnp.int32)[None, :]).astype(
        jnp.int32
    )
    starts = brick_offsets[0]
    quarter_start = lax.axis_index("slab") % ZQ * SLAB_Z
    start_z = starts[0] + quarter_start
    bricks = source_bricks[0]
    want_local = lax.all_to_all(
        (jnp.sum(slot_hits * (local_index[:, None] + 1), axis=0) - 1).reshape(slab_count, capacity),
        "slab",
        split_axis=0,
        concat_axis=0,
        tiled=True,
    )
    picked = bricks[jnp.clip(want_local.reshape(-1), 0, held_count - 1)]
    arrived = lax.all_to_all(
        picked.reshape(slab_count, capacity, -1), "slab", split_axis=0, concat_axis=0, tiled=True
    )
    padded = arrived.reshape(slot_count, -1)[slot_of]
    own_pieces = jax.vmap(crop_window)(padded, start_z, starts[1], starts[2])
    width_x = deformation.shape[4]
    across = width_x // BRICK
    rows_y = pieces_here // across
    voxel_field = own_pieces.reshape(rows_y, across, COMP, SLAB_Z, BRICK, BRICK)
    voxel_field = voxel_field.transpose(2, 3, 0, 4, 1, 5).reshape(
        COMP, SLAB_Z, rows_y * BRICK, width_x
    )
    rimmed = extended(deformation[0].astype(jnp.bfloat16), (("slab", 1),), 1).astype(jnp.float32)
    rimmed = jnp.pad(rimmed, ((0, 0), (0, 0), (1, 1), (1, 1)))
    rotation = polar_factor(jacobian(rimmed))
    tensor = voxel_field.astype(jnp.float32)
    rotated = jnp.stack(reorient([tensor[channel] for channel in range(COMP)], rotation))
    summed = lax.psum_scatter(rotated, "subj", scatter_dimension=2, tiled=True)
    return summed / lax.axis_size("subj")


def solution(mesh):
    in_specs = (
        P("subj", "slab", None),
        P("subj", "slab"),
        P("subj", None, "slab"),
        P("subj", None, "slab", None, None),
    )
    out_specs = P(None, "slab", "subj", None)
    return jax.shard_map(shards, mesh=mesh, in_specs=in_specs, out_specs=out_specs, check_vma=False)
```

profile of v0, /device:TPU:0, one launch (start us, length us, event | category | flops | bytes accessed | tf_op | source)
XLA Modules:
  0.0 446.8 jit_solution(1695607794835001815)
XLA Ops:
  8.3 11.7 %all_to_all.11 = s32[8,1,6]{2,1,0:T(1,128)S(1)} all-to-all(s32[8,1,6]{2,1,0:T(1,128)S(1)} %bitcast.75), channel_id=1, replica_groups=mesh['subj'=4,'slab'=8] {'slab'}, dimensions={0} | all-to-all | bytes 384 | tf_op jit(solution)/shard_map/all_to_all | solution.py:126
  20.1 5.8 %gather_fusion = bf16[48,48000]{1,0:T(8,128)(2,1)} fusion(bf16[8,48000]{1,0:T(8,128)(2,1)S(1)} %bitcast.73, s32[1024]{0:T(1024)S(1)} %pad_clamp_fusion.1), kind=kCustom, calls=%fused_computation | custom fusion | bytes 9216192 | tf_op jit(solution)/shard_map/gather | solution.py:133
  25.9 5.1 %reshape.276 = bf16[8,6,48000]{2,1,0:T(8,128)(2,1)} reshape(bf16[48,48000]{1,0:T(8,128)(2,1)} %gather_fusion) | data formatting | bytes 9216000 | tf_op jit(solution)/shard_map/reshape | solution.py:135
  31.0 4.9 %all-to-all-start.1 = ((bf16[8,6,48000]{2,1,0:T(8,128)(2,1)}), bf16[8,6,48000]{2,1,0:T(8,128)(2,1)}, u32[]{:S(2)}, u32[]{:S(2)}) async-start(bf16[8,6,48000]{2,1,0:T(8,128)(2,1)} %reshape.276), calls=%async_computation.1 | async-start | bytes 12288000 | tf_op jit(solution)/shard_map/all_to_all | solution.py:134
  36.0 2.2 collective-permute-start
  39.7 2.8 collective-permute-done.1
  45.0 126.7 %all-to-all-done.1 = bf16[8,6,48000]{2,1,0:T(8,128)(2,1)} async-done(((bf16[8,6,48000]{2,1,0:T(8,128)(2,1)}), bf16[8,6,48000]{2,1,0:T(8,128)(2,1)}, u32[]{:S(2)}, u32[]{:S(2)}) %all-to-all-start.1) | async-done | bytes 4608032 | tf_op jit(solution)/shard_map/all_to_all | solution.py:134
  171.7 5.1 %reshape.277 = bf16[48,48000]{1,0:T(8,128)(2,1)} reshape(bf16[8,6,48000]{2,1,0:T(8,128)(2,1)} %all-to-all-done.1) | data formatting | bytes 9216000 | tf_op jit(solution)/shard_map/reshape | solution.py:137
  176.8 9.7 %gather_fusion.1 = bf16[32,48000]{1,0:T(8,128)(2,1)} fusion(bf16[48,48000]{1,0:T(8,128)(2,1)} %reshape.277, s32[1024]{0:T(1024)S(1)} %pad_clamp_fusion), kind=kCustom, calls=%fused_computation.1 | custom fusion | bytes 6144128 | tf_op jit(solution)/shard_map/gather | solution.py:137
  186.5 39.6 %reshape.278 = bf16[32,6,20,20,20]{4,3,2,1,0:T(8,128)(2,1)} reshape(bf16[32,48000]{1,0:T(8,128)(2,1)} %gather_fusion.1) | data formatting | bytes 6144000 | tf_op jit(solution)/shard_map/vmap()/reshape | solution.py:33
  226.1 150.6 %while.1 = (s32[]{:T(128)}, bf16[32,6,20,20,20]{4,3,2,1,0:T(8,128)(2,1)}, s32[32,5]{0,1:T(8,128)S(1)}, bf16[32,6,4,16,16]{4,3,2,1,0:T(8,128)(2,1)}, s32[]{:T(128)}) while((s32[]{:T(128)}, bf16[32,6,20,20,20]{4,3,2,1,0:T(8,128)(2,1)}, s32[32,5]{0,1:T(8,128)S(1)}, bf16[32,6,4,16,16]{4,3,2,1,0:T(8,128)(2,1)}, s32[]{:T(128)}) %tuple.65), condition=%wide.while_cond, body=%wide.while_body.sunk | while | flops 2 | bytes 199305 | solution.py:35
  226.8 4.0 dynamic-slice_dynamic-update-slice_fusion.2
  231.5 4.0 dynamic-slice_dynamic-update-slice_fusion.2
  236.2 4.0 dynamic-slice_dynamic-update-slice_fusion.2
  240.9 4.0 dynamic-slice_dynamic-update-slice_fusion.2
  245.6 4.0 dynamic-slice_dynamic-update-slice_fusion.2
  250.3 4.0 dynamic-slice_dynamic-update-slice_fusion.2
  255.0 4.0 dynamic-slice_dynamic-update-slice_fusion.2
  259.7 4.0 dynamic-slice_dynamic-update-slice_fusion.2
  264.4 4.0 dynamic-slice_dynamic-update-slice_fusion.2
  269.1 4.0 dynamic-slice_dynamic-update-slice_fusion.2
  273.8 4.0 dynamic-slice_dynamic-update-slice_fusion.2
  278.5 4.0 dynamic-slice_dynamic-update-slice_fusion.2
  283.3 4.1 dynamic-slice_dynamic-update-slice_fusion.2
  288.0 4.0 dynamic-slice_dynamic-update-slice_fusion.2
  292.7 4.0 dynamic-slice_dynamic-update-slice_fusion.2
  297.4 4.0 dynamic-slice_dynamic-update-slice_fusion.2
  302.1 4.0 dynamic-slice_dynamic-update-slice_fusion.2
  306.8 4.0 dynamic-slice_dynamic-update-slice_fusion.2
  311.5 4.0 dynamic-slice_dynamic-update-slice_fusion.2
  316.2 4.0 dynamic-slice_dynamic-update-slice_fusion.2
  320.9 4.0 dynamic-slice_dynamic-update-slice_fusion.2
  325.6 4.0 dynamic-slice_dynamic-update-slice_fusion.2
  330.3 4.0 dynamic-slice_dynamic-update-slice_fusion.2
  335.0 4.0 dynamic-slice_dynamic-update-slice_fusion.2
  339.7 4.0 dynamic-slice_dynamic-update-slice_fusion.2
  344.4 4.0 dynamic-slice_dynamic-update-slice_fusion.2
  349.2 4.0 dynamic-slice_dynamic-update-slice_fusion.2
  353.9 4.0 dynamic-slice_dynamic-update-slice_fusion.2
  358.6 4.0 dynamic-slice_dynamic-update-slice_fusion.2
  363.3 4.0 dynamic-slice_dynamic-update-slice_fusion.2
  368.0 4.0 dynamic-slice_dynamic-update-slice_fusion.2
  372.7 4.0 dynamic-slice_dynamic-update-slice_fusion.2
  376.7 2.7 convert_bitcast_fusion
  384.6 2.8 copy.30
  388.9 2.8 copy.31
  393.3 2.8 copy.32
  411.2 27.1 %reduce-scatter.2.cloned.1.call-done = f32[6,4,16,128]{3,2,1,0:T(8,128)} async-done(((f32[6,4,64,128]{3,2,1,0:T(8,128)}), f32[6,4,16,128]{3,2,1,0:T(8,128)}) %reduce-scatter.2.cloned.1.call-update) | async-done | bytes 196624 | tf_op jit(solution)/shard_map/reduce_scatter | solution.py:151
  (140 shorter events, 52.1 us)
Async XLA Ops:
  6.5 13.6 %copy-start = (bf16[1,8,48000]{2,1,0:T(8,128)(2,1)S(1)}, bf16[1,8,48000]{2,1,0:T(8,128)(2,1)}, u32[]{:S(2)}) copy-start(bf16[1,8,48000]{2,1,0:T(8,128)(2,1)} %param.4) | copy-start | bytes 2304004
  31.0 4.9 %copy-start.12 = (f32[1,3,4,64,128]{4,3,2,1,0:T(8,128)S(1)}, f32[1,3,4,64,128]{4,3,2,1,0:T(8,128)}, u32[]{:S(2)}) copy-start(f32[1,3,4,64,128]{4,3,2,1,0:T(8,128)} %param.7) | copy-start | bytes 1179652
  31.0 8.6 %copy-start.14 = (s32[1,32]{1,0:T(1,128)S(1)}, s32[1,32]{1,0:T(1,128)}, u32[]{:S(2)}) copy-start(s32[1,32]{1,0:T(1,128)} %param.5) | copy-start | bytes 388
  31.0 8.6 %copy-start.13 = (s32[1,3,32]{2,0,1:T(1,128)S(1)}, s32[1,3,32]{2,0,1:T(1,128)}, u32[]{:S(2)}) copy-start(s32[1,3,32]{2,0,1:T(1,128)} %param.6) | copy-start | bytes 1156
  31.0 140.7 %all-to-all-start.1 = ((bf16[8,6,48000]{2,1,0:T(8,128)(2,1)}), bf16[8,6,48000]{2,1,0:T(8,128)(2,1)}, u32[]{:S(2)}, u32[]{:S(2)}) async-start(bf16[8,6,48000]{2,1,0:T(8,128)(2,1)} %reshape.276), calls=%async_computation.1 | async-start | bytes 12288000 | tf_op jit(solution)/shard_map/all_to_all | solution.py:134
  35.9 402.5 %reduce-scatter.2.cloned.1.call-start = ((), (), s32[]{:S(2)}) async-start(), calls=%async_computation.3 | async-start | bytes 983040 | tf_op jit(solution)/shard_map/reduce_scatter | solution.py:151
  36.0 3.7 collective-permute-start
  38.2 4.3 collective-permute-start.1
  43.1 361.8 %copy-start.2 = (f32[1,4,64,128]{3,2,1,0:T(8,128)}, f32[1,4,64,128]{3,2,1,0:T(8,128)S(1)}, u32[]{:S(2)}) copy-start(f32[1,4,64,128]{3,2,1,0:T(8,128)S(1)} %get-tuple-element.67) | copy-start | bytes 393220
  43.1 361.8 %copy-start.3 = (f32[1,4,64,128]{3,2,1,0:T(8,128)}, f32[1,4,64,128]{3,2,1,0:T(8,128)S(1)}, u32[]{:S(2)}) copy-start(f32[1,4,64,128]{3,2,1,0:T(8,128)S(1)} %get-tuple-element.68) | copy-start | bytes 393220
  44.2 360.8 %copy-start.4 = (f32[1,4,64,128]{3,2,1,0:T(8,128)}, f32[1,4,64,128]{3,2,1,0:T(8,128)S(1)}, u32[]{:S(2)}) copy-start(f32[1,4,64,128]{3,2,1,0:T(8,128)S(1)} %get-tuple-element.56) | copy-start | bytes 393220
  44.2 360.8 %copy-start.5 = (f32[1,4,64,128]{3,2,1,0:T(8,128)}, f32[1,4,64,128]{3,2,1,0:T(8,128)S(1)}, u32[]{:S(2)}) copy-start(f32[1,4,64,128]{3,2,1,0:T(8,128)S(1)} %get-tuple-element.59) | copy-start | bytes 393220
  44.2 360.8 %copy-start.6 = (f32[1,4,64,128]{3,2,1,0:T(8,128)}, f32[1,4,64,128]{3,2,1,0:T(8,128)S(1)}, u32[]{:S(2)}) copy-start(f32[1,4,64,128]{3,2,1,0:T(8,128)S(1)} %get-tuple-element.63) | copy-start | bytes 393220
  402.6 4.3 copy-start.7
  402.6 4.3 copy-start.8
  402.6 4.3 copy-start.9
  402.7 4.3 copy-start.10
  402.7 4.3 copy-start.11
  407.0 33.0 %copy-start.1 = (bf16[1,8,48000]{2,1,0:T(8,128)(2,1)S(1)}, bf16[1,8,48000]{2,1,0:T(8,128)(2,1)}, u32[]{:S(2)}) copy-start(bf16[1,8,48000]{2,1,0:T(8,128)(2,1)} %param.4) | copy-start | bytes 2304004
Sparse Core Ops, SparseCore 0:
  411.3 26.9 reduce-scatter.1
where the time goes:
time: 449 us; the launch traced here: 447 us
  local copies, waits for them, and re-layouts  240 us (53%)
  waiting for transfers between devices  157 us (35%)
  other arithmetic  16.6 us (4%)
  between operations  13.7 us (3%)
  blocking collectives  11.7 us (3%)
  starting transfers between devices  8.45 us (2%)
    gather x96, local copies, waits for them, and re-layouts  151 us
    all_to_all x1, waiting for transfers between devices, shards(): lax.all_to_all(picked.reshape(slab_count, capacity, -1), 'slab', split_ax...  127 us
    reshape x1, local copies, waits for them, and re-layouts, crop_window(): brick_cube = flat_brick.reshape(COMP, edge_full, edge_full, edge_full)  39.6 us
    reduce_scatter x1, waiting for transfers between devices, shards(): summed = lax.psum_scatter(rotated, 'subj', scatter_dimension=2, tiled=True)  27.1 us
    slice x13, local copies, waits for them, and re-layouts, shards(): tensor[channel]  23.5 us
    all_to_all x1, blocking collectives, shards(): lax.all_to_all((jnp.sum(slot_hits * (local_index[:, None] + 1), axis=0) -...  11.7 us
    gather x1, local copies, waits for them, and re-layouts, shards(): padded = arrived.reshape(slot_count, -1)[slot_of]  9.7 us
  transfers between devices with their start and end apart: 4, of which 3 were waited for; matrix products, arithmetic and copies ran while one was open for 1% of the time, Pallas kernels for 0%

commit v1 on v0

v1 whole, which is shorter than its diff:
```python
import functools

import jax
import jax.numpy as jnp
from jax import lax
from jax.experimental import pallas as pl
from jax.experimental.pallas import tpu as pltpu
from jax.sharding import PartitionSpec as P

COMP = 6
BRICK = 16
PAD = 2
EDGE = BRICK + 2 * PAD
ZQ = 4
NEWTON = 2
SLAB_Z = 4
LANES = 128
ROWS = COMP * SLAB_Z
BRICK_ROWS = COMP * EDGE
SPAN = 384
FLAT = BRICK * BRICK


def relayout_bricks(x_ref, rows_ref):
    held = x_ref.shape[0]
    lane = lax.broadcasted_iota(jnp.int32, (held, LANES), 1)
    group_lanes = 8 * EDGE * EDGE
    for group in range(BRICK_ROWS // 8):
        for m in range(8):
            cz = group * 8 + m
            c, z = cz // EDGE, cz % EDGE
            first = group * group_lanes + 3 * m * LANES
            shift = 16 * m
            tiles = []
            for j in range(4):
                tile = x_ref[:, first + j * LANES:first + (j + 1) * LANES].astype(jnp.float32)
                tiles.append(pltpu.roll(tile, LANES - shift, 1) if shift else tile)
            for j in range(4):
                value = tiles[j]
                if shift and j < 3:
                    value = jnp.where(lane < LANES - shift, tiles[j], tiles[j + 1])
                rows_ref[j, pl.ds(z * COMP + c, held, stride=BRICK_ROWS), :] = value


def selection():
    source = lax.broadcasted_iota(jnp.int32, (SPAN, FLAT), 0)
    target = lax.broadcasted_iota(jnp.int32, (SPAN, FLAT), 1)
    return (source == target // BRICK * EDGE + target % BRICK).astype(jnp.float32).astype(jnp.bfloat16)


def shifted_window(rows_ref, code):
    start, shift = code // LANES, code % LANES
    lane = lax.broadcasted_iota(jnp.int32, (ROWS, LANES), 1)
    rolled = [
        pltpu.roll(rows_ref[j, pl.ds(start, ROWS), :], (LANES - shift) % LANES, 1) for j in range(4)
    ]
    return [jnp.where(lane < LANES - shift, rolled[j], rolled[j + 1]) for j in range(3)]


def crop_kernel(code_ref, x_ref, out_ref, rows_ref, shifted_ref):
    relayout_bricks(x_ref, rows_ref)
    readers, chunk, _ = out_ref.shape
    capacity = chunk // ROWS
    select = selection()

    def step(reader, carry):
        for slot in range(capacity):
            window = shifted_window(rows_ref, code_ref[reader * capacity + slot])
            for j in range(3):
                shifted_ref[slot * ROWS:(slot + 1) * ROWS, j * LANES:(j + 1) * LANES] = window[j]
        out_ref[reader] = jnp.dot(
            shifted_ref[...].astype(jnp.bfloat16), select, preferred_element_type=jnp.float32
        ).astype(jnp.bfloat16)
        return carry

    lax.fori_loop(0, readers, step, 0)


def swap_groups(value):
    sub = lax.broadcasted_iota(jnp.int32, value.shape, 1)
    group = lax.broadcasted_iota(jnp.int32, value.shape, 2) // BRICK
    for bit in (1, 2, 4):
        from_below = pltpu.roll(pltpu.roll(value, 8 - bit, 1), BRICK * bit, 2)
        if bit == 4:
            from_above = from_below
        else:
            from_above = pltpu.roll(pltpu.roll(value, bit, 1), LANES - BRICK * bit, 2)
        low = (sub & bit) == 0
        same = (sub & bit) == (group & bit)
        value = jnp.where(same, value, jnp.where(low, from_below, from_above))
    return value


def place_row(slot_ref, wide_ref, turned_ref, row):
    across = LANES // BRICK
    for j in range(across):
        base = pl.multiple_of(slot_ref[row * across + j] * ROWS, 8)
        for h in range(2):
            for part in range(ROWS // 8):
                turned_ref[h, pl.ds(part * 64 + j, 8, stride=8), :] = wide_ref[
                    h, pl.ds(base + part * 8, 8), :
                ]
    return [swap_groups(turned_ref[h].reshape(ROWS, 8, LANES)) for h in range(2)]


def place_kernel(slot_ref, in_ref, out_ref, wide_ref, turned_ref):
    readers, chunk, _ = in_ref.shape

    def widen(reader, carry):
        base = pl.multiple_of(reader * chunk, 8)
        for h in range(2):
            wide_ref[h, pl.ds(base, chunk), :] = in_ref[
                reader, :, h * LANES:(h + 1) * LANES
            ].astype(jnp.float32)
        return carry

    lax.fori_loop(0, readers, widen, 0)

    def step(row, carry):
        halves = place_row(slot_ref, wide_ref, turned_ref, row)
        out_ref[row] = jnp.concatenate(halves, axis=1).astype(jnp.bfloat16)
        return carry

    lax.fori_loop(0, out_ref.shape[0], step, 0)


def polar_factor(matrix):
    for newton_step in range(NEWTON):
        cofactor = [
            [
                matrix[(a + 1) % 3][(b + 1) % 3] * matrix[(a + 2) % 3][(b + 2) % 3]
                - matrix[(a + 1) % 3][(b + 2) % 3] * matrix[(a + 2) % 3][(b + 1) % 3]
                for b in range(3)
            ]
            for a in range(3)
        ]
        determinant = (
            matrix[0][0] * cofactor[0][0]
            + matrix[0][1] * cofactor[0][1]
            + matrix[0][2] * cofactor[0][2]
        )
        scaling = 0.5 / determinant
        matrix = [
            [0.5 * matrix[a][b] + cofactor[a][b] * scaling for b in range(3)] for a in range(3)
        ]
    return matrix


def reorient(components, rotation):
    tensor_rows = [
        [components[0], components[3], components[4]],
        [components[3], components[1], components[5]],
        [components[4], components[5], components[2]],
    ]
    left_side = [
        [
            rotation[a][0] * tensor_rows[0][b]
            + rotation[a][1] * tensor_rows[1][b]
            + rotation[a][2] * tensor_rows[2][b]
            for b in range(3)
        ]
        for a in range(3)
    ]
    pair_list = ((0, 0), (1, 1), (2, 2), (0, 1), (0, 2), (1, 2))
    return [
        left_side[a][0] * rotation[b][0]
        + left_side[a][1] * rotation[b][1]
        + left_side[a][2] * rotation[b][2]
        for a, b in pair_list
    ]


def rotation_at(load):
    lane = lax.broadcasted_iota(jnp.int32, (BRICK, LANES), 1)
    matrix = []
    for a in range(3):
        here = load(a, 1)
        centre = here[1:BRICK + 1]
        along_z = (load(a, 2)[1:BRICK + 1] - load(a, 0)[1:BRICK + 1]) * 0.5
        along_y = (here[2:BRICK + 2] - here[0:BRICK]) * 0.5
        later = jnp.where(lane == LANES - 1, 0.0, pltpu.roll(centre, LANES - 1, 1))
        earlier = jnp.where(lane == 0, 0.0, pltpu.roll(centre, 1, 1))
        gradients = [along_z, along_y, (later - earlier) * 0.5]
        gradients[a] = gradients[a] + 1.0
        matrix.append(gradients)
    return polar_factor(matrix)


def mean_kernel(field_ref, u_ref, out_ref):
    subjects = field_ref.shape[0]

    def step(z, carry):
        total = None
        for s in range(subjects):
            rotation = rotation_at(lambda a, dz: u_ref[s, a, z + dz].astype(jnp.float32))
            tensor = [field_ref[s, z * COMP + c].astype(jnp.float32) for c in range(COMP)]
            rotated = reorient(tensor, rotation)
            total = rotated if total is None else [p + q for p, q in zip(total, rotated)]
        for c in range(COMP):
            out_ref[c, z] = total[c] * (1.0 / subjects)
        return carry

    lax.fori_loop(0, SLAB_Z, step, 0)


VMEM_SPEC = pl.BlockSpec(memory_space=pltpu.VMEM)
SMEM_SPEC = pl.BlockSpec(memory_space=pltpu.SMEM)
PARAMS = pltpu.CompilerParams(vmem_limit_bytes=40 << 20)


def slot_tables(brick_ids, brick_offsets, held, slab_count, capacity):
    wanted = brick_ids[0]
    pieces = wanted.shape[0]
    owner, local = wanted // held, wanted % held
    positions = jnp.arange(pieces, dtype=jnp.int32)
    earlier = (owner[:, None] == owner[None, :]) & (positions[None, :] < positions[:, None])
    slot_of = owner * capacity + jnp.sum(earlier.astype(jnp.int32), axis=1)
    start_z = brick_offsets[0, 0] + lax.axis_index("slab") % ZQ * SLAB_Z
    shift = brick_offsets[0, 1] * EDGE + brick_offsets[0, 2]
    code = (local * BRICK_ROWS + start_z * COMP) * LANES + shift
    hits = slot_of[:, None] == jnp.arange(slab_count * capacity, dtype=jnp.int32)[None, :]
    return slot_of, jnp.sum(jnp.where(hits, code[:, None], 0), axis=0)


def row_windows(deformation, subjects):
    u = deformation[0].astype(jnp.bfloat16)
    count = lax.axis_size("slab")
    before = lax.ppermute(u[:, -1:], "slab", [(i, i + 1) for i in range(count - 1)])
    after = lax.ppermute(u[:, :1], "slab", [(i + 1, i) for i in range(count - 1)])
    u = jnp.concatenate([before, u, after], axis=1)
    u = jnp.pad(u, ((0, 0), (0, 0), (1, 1), (0, 0)))
    blocks = jnp.stack([u[:, :, r * BRICK:r * BRICK + BRICK + 2] for r in range(subjects)])
    return lax.all_to_all(blocks, "subj", split_axis=0, concat_axis=0, tiled=True)


def shards(source_bricks, brick_ids, brick_offsets, deformation):
    slab_count, subjects = lax.axis_size("slab"), lax.axis_size("subj")
    pieces = brick_ids.shape[1]
    held = source_bricks.shape[1]
    capacity = max(2, 3 * pieces // (2 * slab_count))
    chunk = capacity * ROWS
    slot_of, code = slot_tables(brick_ids, brick_offsets, held, slab_count, capacity)
    asked = lax.all_to_all(
        code.reshape(slab_count, capacity), "slab", split_axis=0, concat_axis=0, tiled=True
    ).reshape(-1)
    rows = row_windows(deformation, subjects)
    cropped = pl.pallas_call(
        crop_kernel,
        out_shape=jax.ShapeDtypeStruct((slab_count, chunk, FLAT), jnp.bfloat16),
        in_specs=[SMEM_SPEC, VMEM_SPEC],
        out_specs=VMEM_SPEC,
        scratch_shapes=[
            pltpu.VMEM((4, held * BRICK_ROWS, LANES), jnp.float32),
            pltpu.VMEM((chunk, SPAN), jnp.float32),
        ],
        compiler_params=PARAMS,
    )(asked, source_bricks[0])
    arrived = lax.all_to_all(cropped, "slab", split_axis=0, concat_axis=0, tiled=True)
    rows_y = pieces // (deformation.shape[4] // BRICK)
    placed = pl.pallas_call(
        place_kernel,
        out_shape=jax.ShapeDtypeStruct((rows_y, ROWS, BRICK, LANES), jnp.bfloat16),
        in_specs=[SMEM_SPEC, VMEM_SPEC],
        out_specs=VMEM_SPEC,
        scratch_shapes=[
            pltpu.VMEM((2, slab_count * chunk, LANES), jnp.float32),
            pltpu.VMEM((2, ROWS * 8, LANES), jnp.float32),
        ],
        compiler_params=PARAMS,
    )(slot_of, arrived)
    fields = lax.all_to_all(placed, "subj", split_axis=0, concat_axis=0, tiled=True)
    return pl.pallas_call(
        mean_kernel,
        out_shape=jax.ShapeDtypeStruct((COMP, SLAB_Z, BRICK, LANES), jnp.float32),
        in_specs=[VMEM_SPEC, VMEM_SPEC],
        out_specs=VMEM_SPEC,
        compiler_params=PARAMS,
    )(fields, rows)


def solution(mesh):
    in_specs = (
        P("subj", "slab", None),
        P("subj", "slab"),
        P("subj", None, "slab"),
        P("subj", None, "slab", None, None),
    )
    out_specs = P(None, "slab", "subj", None)
    return jax.shard_map(shards, mesh=mesh, in_specs=in_specs, out_specs=out_specs, check_vma=False)
```

time: 449 us -> 62.9 us (0.14)
  local copies, waits for them, and re-layouts: 240 us -> 2.65 us
  waiting for transfers between devices: 157 us -> 16.9 us
  other arithmetic: 16.6 us -> 1.88 us
  between operations: 13.7 us -> 0.09 us
  Pallas kernels: 0 us -> 9.3 us
  blocking collectives: 11.7 us -> 20.7 us
    gather x99 -> x0, local copies, waits for them, and re-layouts: 166 us -> none
    all_to_all x1 -> x2, waiting for transfers between devices: 127 us -> 14 us  [the longest x1 9 us: shards(): lax.all_to_all(cropped, 'slab', split_axis=0, concat_axis=0, tiled=True)]
    reshape x3 -> x1, local copies, waits for them, and re-layouts: 49.8 us -> 0.08 us  [shards(): asked = lax.all_to_all(code.reshape(slab_count, capacity), 'slab', split_...]
    reduce_scatter x1 -> x0, waiting for transfers between devices: 27.1 us -> none  [shards(): summed = lax.psum_scatter(rotated, 'subj', scatter_dimension=2, tiled=True)]
    slice x14 -> x1, local copies, waits for them, and re-layouts: 23.5 us -> 0.01 us  [row_windows(): u[:, -1:]]
    pallas_call x0 -> x3, Pallas kernels: none -> 9.3 us  [the longest x1 3.91 us: shards(): pl.pallas_call(crop_kernel, out_shape=jax.ShapeDtypeStruct((slab_count, c...]
    all_to_all x1 -> x2, blocking collectives: 11.7 us -> 20.7 us  [the longest x1 11.7 us: shards(): lax.all_to_all(code.reshape(slab_count, capacity), 'slab', split_axis=0,...]
    unnamed x6 -> x0, other arithmetic: 7.41 us -> none
  transfers between devices with their start and end apart: 4 -> 4, of which waited for: 3 -> 3; matrix products, arithmetic and copies ran while one was open for 1% -> 2% of each run, Pallas kernels for 0% -> 3%
where the time goes in v1:
time: 62.9 us; the launch traced here: 62.5 us
  blocking collectives  20.7 us (33%)
  waiting for transfers between devices  16.9 us (27%)
  starting transfers between devices  11 us (17%)
  Pallas kernels  9.3 us (15%)
  local copies, waits for them, and re-layouts  2.65 us (4%)
  other arithmetic  1.88 us (3%)
    all_to_all x1, blocking collectives, shards(): lax.all_to_all(code.reshape(slab_count, capacity), 'slab', split_axis=0,...  11.7 us
    all_to_all x1, waiting for transfers between devices, shards(): lax.all_to_all(cropped, 'slab', split_axis=0, concat_axis=0, tiled=True)  9 us
    all_to_all x1, blocking collectives, shards(): lax.all_to_all(placed, 'subj', split_axis=0, concat_axis=0, tiled=True)  8.99 us
    all_to_all x1, waiting for transfers between devices, row_windows(): lax.all_to_all(blocks, 'subj', split_axis=0, concat_axis=0, tiled=True)  4.96 us
    pallas_call x1, Pallas kernels, shards(): pl.pallas_call(crop_kernel, out_shape=jax.ShapeDtypeStruct((slab_count, c...  3.91 us
    all_to_all x1, starting transfers between devices, row_windows(): lax.all_to_all(blocks, 'subj', split_axis=0, concat_axis=0, tiled=True)  3.72 us
    all_to_all x1, starting transfers between devices, shards(): lax.all_to_all(cropped, 'slab', split_axis=0, concat_axis=0, tiled=True)  3.67 us
    pallas_call x1, Pallas kernels, shards(): pl.pallas_call(mean_kernel, out_shape=jax.ShapeDtypeStruct((COMP, SLAB_Z,...  3.46 us
  transfers between devices with their start and end apart: 4, of which 3 were waited for; matrix products, arithmetic and copies ran while one was open for 2% of the time, Pallas kernels for 3%

profile of v1, /device:TPU:0, one launch (start us, length us, event | category | flops | bytes accessed | tf_op | source)
XLA Modules:
  0.0 62.5 jit_solution(10144389059369734292)
XLA Ops:
  0.0 0.0 copy-start.3
  0.0 0.0 copy-start.2
  0.0 0.7 %copy-done.3 = s32[1,32]{1,0:T(1,128)S(1)} copy-done((s32[1,32]{1,0:T(1,128)S(1)}, s32[1,32]{1,0:T(1,128)}, u32[]{:S(2)}) %copy-start.3) | copy-done | bytes 152
  0.7 0.0 copy-done.2
  0.7 0.2 convert_reduce_fusion
  0.9 0.1 select_reduce_fusion
  1.0 0.1 all_to_all.15
  1.1 11.7 %all_to_all.24 = s32[8,1,6]{2,1,0:T(1,128)S(1)} all-to-all(s32[8,1,6]{2,1,0:T(1,128)S(1)} %bitcast.36), channel_id=1, replica_groups=mesh['subj'=4,'slab'=8] {'slab'}, dimensions={0} | all-to-all | bytes 384 | tf_op jit(solution)/shard_map/all_to_all | solution.py:243
  12.8 0.5 broadcast.143
  13.3 0.7 %reduce.3 = s32[8,6]{1,0:T(8,128)S(1)} reduce(s32[8,1,6]{2,1,0:T(1,128)S(1)} %all_to_all.24, s32[]{:T(128)} %broadcast.143), dimensions={1}, to_apply=%all_to_all.16.reduce_sub_computation.3 | reduce | bytes 388 | tf_op jit(solution)/shard_map/all_to_all | solution.py:243
  13.9 0.1 reshape.98.code_ref
  14.0 0.0 copy-start
  14.0 1.1 %copy-done = bf16[1,8,48000]{2,1,0:T(8,128)(2,1)S(1)} copy-done((bf16[1,8,48000]{2,1,0:T(8,128)(2,1)S(1)}, bf16[1,8,48000]{2,1,0:T(8,128)(2,1)}, u32[]{:S(2)}) %copy-start) | copy-done | bytes 768024
  15.1 3.9 %shard_map.46 = bf16[8,144,256]{2,1,0:T(8,128)(2,1)} custom-call(s32[48]{0:T(128)S(1)} %reshape.98.code_ref, bf16[8,48000]{1,0:T(8,128)(2,1)S(1)} %bitcast.35), custom_call_target="tpu_custom_call" | custom-call | tf_op jit(solution)/shard_map/pallas_call | solution.py:247
  19.1 0.0 copy-start.1
  19.1 3.7 %all-to-all-start.1 = ((bf16[8,144,256]{2,1,0:T(8,128)(2,1)}), bf16[8,144,256]{2,1,0:T(8,128)(2,1)S(1)}, u32[]{:S(2)}, u32[]{:S(2)}) async-start(bf16[8,144,256]{2,1,0:T(8,128)(2,1)} %shard_map.46), calls=%async_computation.1 | async-start | bytes 1179648 | tf_op jit(solution)/shard_map/all_to_all | solution.py:258
  22.7 0.0 copy-done.1
  22.8 2.3 %collective-permute-start = (bf16[3,1,64,128]{3,2,1,0:T(8,128)(2,1)S(1)}, bf16[3,1,64,128]{3,2,1,0:T(8,128)(2,1)S(1)}, u32[]{:S(2)}, u32[]{:S(2)}) collective-permute-start(bf16[3,1,64,128]{3,2,1,0:T(8,128)(2,1)S(1)} %get-tuple-element.9), channel_id=1, source_target_pairs={{0,1},{1,2},{2,3},{3,4},{4,5},{5,6},{6,7},{8,9},{9,10},{10,11},{11... | collective-permute-start | bytes 147464 | tf_op jit(solution)/shard_map/ppermute | solution.py:228
  25.1 1.3 %collective-permute-start.1 = (bf16[3,1,64,128]{3,2,1,0:T(8,128)(2,1)S(1)}, bf16[3,1,64,128]{3,2,1,0:T(8,128)(2,1)S(1)}, u32[]{:S(2)}, u32[]{:S(2)}) collective-permute-start(bf16[3,1,64,128]{3,2,1,0:T(8,128)(2,1)S(1)} %get-tuple-element.10), channel_id=1, source_target_pairs={{1,0},{2,1},{3,2},{4,3},{5,4},{6,5},{7,6},{9,8},{10,9},{11,10},{12... | collective-permute-start | bytes 147464 | tf_op jit(solution)/shard_map/ppermute | solution.py:229
  26.4 0.0 collective-permute-done
  26.4 3.0 %collective-permute-done.1 = bf16[3,1,64,128]{3,2,1,0:T(8,128)(2,1)S(1)} collective-permute-done((bf16[3,1,64,128]{3,2,1,0:T(8,128)(2,1)S(1)}, bf16[3,1,64,128]{3,2,1,0:T(8,128)(2,1)S(1)}, u32[]{:S(2)}, u32[]{:S(2)}) %collective-permute-start.1) | collective-permute-done | bytes 49184 | tf_op jit(solution)/shard_map/ppermute | solution.py:229
  29.4 0.2 fusion
  29.6 0.8 %pad_maximum_fusion = bf16[4,3,6,18,128]{4,3,2,1,0:T(8,128)(2,1)} fusion(bf16[1,3,6,18,128]{4,3,2,1,0:T(8,128)(2,1)S(1)} %get-tuple-element.6, bf16[1,3,6,18,128]{4,3,2,1,0:T(8,128)(2,1)S(1)} %get-tuple-element.7, bf16[1,3,6,18,128]{4,3,2,1,0:T(8,128)(2,1)S(1)} %get-tuple-element.8, bf16[1,3,6,18,128]{4,3,2,1,0:T(8,128)(2,1)S(1)} %get-tuple-element.5), kind=kLoop, calls=%fused_computation | loop fusion | flops 497664 | bytes 663552 | tf_op jit(solution)/shard_map/stack | solution.py:232
  30.4 9.0 %all-to-all-done.1.in_ref = bf16[8,144,256]{2,1,0:T(8,128)(2,1)S(1)} async-done(((bf16[8,144,256]{2,1,0:T(8,128)(2,1)}), bf16[8,144,256]{2,1,0:T(8,128)(2,1)S(1)}, u32[]{:S(2)}, u32[]{:S(2)}) %all-to-all-start.1) | async-done | bytes 589856 | tf_op jit(solution)/shard_map/all_to_all | solution.py:258
  39.4 3.7 %all-to-all-start.3 = ((bf16[4,3,6,18,128]{4,3,2,1,0:T(8,128)(2,1)}), bf16[4,3,6,18,128]{4,3,2,1,0:T(8,128)(2,1)S(1)}, u32[]{:S(2)}, u32[]{:S(2)}) async-start(bf16[4,3,6,18,128]{4,3,2,1,0:T(8,128)(2,1)} %pad_maximum_fusion), calls=%async_computation.3 | async-start | bytes 884736 | tf_op jit(solution)/shard_map/all_to_all | solution.py:233
  43.1 1.9 %shard_map.47 = bf16[4,24,16,128]{3,2,1,0:T(8,128)(2,1)S(1)} custom-call(s32[32]{0:T(128)S(1)} %multiply_add_fusion.slot_ref, bf16[8,144,256]{2,1,0:T(8,128)(2,1)S(1)} %all-to-all-done.1.in_ref), custom_call_target="tpu_custom_call" | custom-call | tf_op jit(solution)/shard_map/pallas_call | solution.py:260
  45.1 5.0 %all-to-all-done.3.u_ref = bf16[4,3,6,18,128]{4,3,2,1,0:T(8,128)(2,1)S(1)} async-done(((bf16[4,3,6,18,128]{4,3,2,1,0:T(8,128)(2,1)}), bf16[4,3,6,18,128]{4,3,2,1,0:T(8,128)(2,1)S(1)}, u32[]{:S(2)}, u32[]{:S(2)}) %all-to-all-start.3) | async-done | bytes 331808 | tf_op jit(solution)/shard_map/all_to_all | solution.py:233
  50.0 9.0 %all_to_all.25.field_ref = bf16[4,24,16,128]{3,2,1,0:T(8,128)(2,1)S(1)} all-to-all(bf16[4,24,16,128]{3,2,1,0:T(8,128)(2,1)S(1)} %shard_map.47), channel_id=1, replica_groups=mesh['subj'=4,'slab'=8] {'subj'}, dimensions={0} | all-to-all | bytes 786432 | tf_op jit(solution)/shard_map/all_to_all | solution.py:271
  59.0 3.5 %shard_map.48 = f32[6,4,16,128]{3,2,1,0:T(8,128)} custom-call(bf16[4,24,16,128]{3,2,1,0:T(8,128)(2,1)S(1)} %all_to_all.25.field_ref, bf16[4,3,6,18,128]{4,3,2,1,0:T(8,128)(2,1)S(1)} %all-to-all-done.3.u_ref), custom_call_target="tpu_custom_call" | custom-call | tf_op jit(solution)/shard_map/pallas_call | solution.py:272
  (6 shorter events, 0.1 us)
Async XLA Ops:
  0.0 0.7 %copy-start.3 = (s32[1,32]{1,0:T(1,128)S(1)}, s32[1,32]{1,0:T(1,128)}, u32[]{:S(2)}) copy-start(s32[1,32]{1,0:T(1,128)} %param.5) | copy-start | bytes 388
  0.0 0.7 %copy-start.2 = (s32[1,3,32]{2,0,1:T(1,128)S(1)}, s32[1,3,32]{2,0,1:T(1,128)}, u32[]{:S(2)}) copy-start(s32[1,3,32]{2,0,1:T(1,128)} %param.6) | copy-start | bytes 1156
  14.0 1.1 %copy-start = (bf16[1,8,48000]{2,1,0:T(8,128)(2,1)S(1)}, bf16[1,8,48000]{2,1,0:T(8,128)(2,1)}, u32[]{:S(2)}) copy-start(bf16[1,8,48000]{2,1,0:T(8,128)(2,1)} %param.4) | copy-start | bytes 2304004
  19.1 3.7 %copy-start.1 = (f32[1,3,4,64,128]{4,3,2,1,0:T(8,128)S(1)}, f32[1,3,4,64,128]{4,3,2,1,0:T(8,128)}, u32[]{:S(2)}) copy-start(f32[1,3,4,64,128]{4,3,2,1,0:T(8,128)} %param.7) | copy-start | bytes 1179652
  19.1 20.4 %all-to-all-start.1 = ((bf16[8,144,256]{2,1,0:T(8,128)(2,1)}), bf16[8,144,256]{2,1,0:T(8,128)(2,1)S(1)}, u32[]{:S(2)}, u32[]{:S(2)}) async-start(bf16[8,144,256]{2,1,0:T(8,128)(2,1)} %shard_map.46), calls=%async_computation.1 | async-start | bytes 1179648 | tf_op jit(solution)/shard_map/all_to_all | solution.py:258
  22.8 3.6 %collective-permute-start = (bf16[3,1,64,128]{3,2,1,0:T(8,128)(2,1)S(1)}, bf16[3,1,64,128]{3,2,1,0:T(8,128)(2,1)S(1)}, u32[]{:S(2)}, u32[]{:S(2)}) collective-permute-start(bf16[3,1,64,128]{3,2,1,0:T(8,128)(2,1)S(1)} %get-tuple-element.9), channel_id=1, source_target_pairs={{0,1},{1,2},{2,3},{3,4},{4,5},{5,6},{6,7},{8,9},{9,10},{10,11},{11... | collective-permute-start | bytes 147464 | tf_op jit(solution)/shard_map/ppermute | solution.py:228
  25.1 4.3 %collective-permute-start.1 = (bf16[3,1,64,128]{3,2,1,0:T(8,128)(2,1)S(1)}, bf16[3,1,64,128]{3,2,1,0:T(8,128)(2,1)S(1)}, u32[]{:S(2)}, u32[]{:S(2)}) collective-permute-start(bf16[3,1,64,128]{3,2,1,0:T(8,128)(2,1)S(1)} %get-tuple-element.10), channel_id=1, source_target_pairs={{1,0},{2,1},{3,2},{4,3},{5,4},{6,5},{7,6},{9,8},{10,9},{11,10},{12... | collective-permute-start | bytes 147464 | tf_op jit(solution)/shard_map/ppermute | solution.py:229
  39.4 10.6 %all-to-all-start.3 = ((bf16[4,3,6,18,128]{4,3,2,1,0:T(8,128)(2,1)}), bf16[4,3,6,18,128]{4,3,2,1,0:T(8,128)(2,1)S(1)}, u32[]{:S(2)}, u32[]{:S(2)}) async-start(bf16[4,3,6,18,128]{4,3,2,1,0:T(8,128)(2,1)} %pad_maximum_fusion), calls=%async_computation.3 | async-start | bytes 884736 | tf_op jit(solution)/shard_map/all_to_all | solution.py:233

commit v2 on v1

v2 whole, which is shorter than its diff:
```python
import jax
import jax.numpy as jnp
from jax import lax
from jax.experimental import pallas as pl
from jax.experimental.pallas import tpu as pltpu
from jax.sharding import PartitionSpec as P

COMP = 6
BRICK = 16
PAD = 2
EDGE = BRICK + 2 * PAD
ZQ = 4
NEWTON = 2
SLAB_Z = 4
LANES = 128
ROWS = COMP * SLAB_Z
BRICK_ROWS = COMP * EDGE
SPAN = 384
FLAT = BRICK * BRICK


def relayout_bricks(x_ref, rows_ref):
    held = x_ref.shape[0]
    lane = lax.broadcasted_iota(jnp.int32, (held, LANES), 1)
    group_lanes = 8 * EDGE * EDGE

    def step(group, carry):
        for m in range(8):
            cz = group * 8 + m
            row = cz % EDGE * COMP + cz // EDGE
            shift = 16 * m
            tiles = []
            for j in range(4):
                first = pl.multiple_of(group * group_lanes + (3 * m + j) * LANES, LANES)
                tile = x_ref[:, pl.ds(first, LANES)].astype(jnp.float32)
                tiles.append(pltpu.roll(tile, LANES - shift, 1) if shift else tile)
            for j in range(4):
                value = tiles[j]
                if shift and j < 3:
                    value = jnp.where(lane < LANES - shift, tiles[j], tiles[j + 1])
                rows_ref[j, pl.ds(row, held, stride=BRICK_ROWS), :] = value
        return carry

    lax.fori_loop(0, BRICK_ROWS // 8, step, 0)


def selection():
    source = lax.broadcasted_iota(jnp.int32, (SPAN, FLAT), 0)
    target = lax.broadcasted_iota(jnp.int32, (SPAN, FLAT), 1)
    return (source == target // BRICK * EDGE + target % BRICK).astype(jnp.float32).astype(jnp.bfloat16)


def crop_rows(codes, capacity, rows, select):
    depth = rows.shape[0]
    row = lax.broadcasted_iota(jnp.int32, (ROWS, depth), 0)
    column = lax.broadcasted_iota(jnp.int32, (ROWS, depth), 1)
    hits, shifts = [], []
    for slot in range(capacity):
        code = codes[:, slot:slot + 1]
        start = lax.shift_right_logical(code, jnp.full(code.shape, 7, jnp.int32))
        hits.append((column - row == jnp.broadcast_to(start, (ROWS, depth))).astype(jnp.float32))
        shifts.append(jnp.broadcast_to(code & (LANES - 1), (ROWS, LANES)))
    hit = jnp.concatenate(hits, axis=0).astype(jnp.bfloat16)
    shift = jnp.concatenate(shifts, axis=0)
    found = jnp.dot(hit, rows, preferred_element_type=jnp.float32)
    tiles = [found[:, j * LANES:(j + 1) * LANES] for j in range(4)]
    for bit in (1, 2, 4, 8, 16, 32, 64):
        taken = (shift & bit) != 0
        tiles = [jnp.where(taken, pltpu.roll(tile, LANES - bit, 1), tile) for tile in tiles]
    inside = lax.broadcasted_iota(jnp.int32, shift.shape, 1) + shift < LANES
    shifted = [jnp.where(inside, tiles[j], tiles[j + 1]).astype(jnp.bfloat16) for j in range(3)]
    return jnp.dot(jnp.concatenate(shifted, axis=1), select, preferred_element_type=jnp.float32)


def swap_groups(value):
    sub = lax.broadcasted_iota(jnp.int32, value.shape, 1)
    group = lax.broadcasted_iota(jnp.int32, value.shape, 2) // BRICK
    for bit in (1, 2, 4):
        from_below = pltpu.roll(pltpu.roll(value, 8 - bit, 1), BRICK * bit, 2)
        if bit == 4:
            from_above = from_below
        else:
            from_above = pltpu.roll(pltpu.roll(value, bit, 1), LANES - BRICK * bit, 2)
        low = (sub & bit) == 0
        same = (sub & bit) == (group & bit)
        value = jnp.where(same, value, jnp.where(low, from_below, from_above))
    return value


def place_row(slot_ref, arrived, row):
    across = LANES // BRICK
    depth = arrived.shape[0] * arrived.shape[1]
    sub = lax.broadcasted_iota(jnp.int32, (8, depth), 0)
    base = jnp.zeros((8, depth), jnp.int32)
    for j in range(across):
        base = jnp.where(sub == j, slot_ref[row * across + j] * ROWS, base)
    offset = lax.broadcasted_iota(jnp.int32, (8, depth), 1) - base
    hit = jnp.concatenate([(offset == n).astype(jnp.float32) for n in range(ROWS)], axis=0)
    pieces = jnp.dot(
        hit.astype(jnp.bfloat16), arrived[...].reshape(depth, FLAT), preferred_element_type=jnp.float32
    )
    return [
        swap_groups(pieces[:, h * LANES:(h + 1) * LANES].reshape(ROWS, 8, LANES)) for h in range(2)
    ]


def polar_factor(matrix):
    for newton_step in range(NEWTON):
        cofactor = [
            [
                matrix[(a + 1) % 3][(b + 1) % 3] * matrix[(a + 2) % 3][(b + 2) % 3]
                - matrix[(a + 1) % 3][(b + 2) % 3] * matrix[(a + 2) % 3][(b + 1) % 3]
                for b in range(3)
            ]
            for a in range(3)
        ]
        determinant = (
            matrix[0][0] * cofactor[0][0]
            + matrix[0][1] * cofactor[0][1]
            + matrix[0][2] * cofactor[0][2]
        )
        scaling = 0.5 / determinant
        matrix = [
            [0.5 * matrix[a][b] + cofactor[a][b] * scaling for b in range(3)] for a in range(3)
        ]
    return matrix


def reorient(components, rotation):
    tensor_rows = [
        [components[0], components[3], components[4]],
        [components[3], components[1], components[5]],
        [components[4], components[5], components[2]],
    ]
    left_side = [
        [
            rotation[a][0] * tensor_rows[0][b]
            + rotation[a][1] * tensor_rows[1][b]
            + rotation[a][2] * tensor_rows[2][b]
            for b in range(3)
        ]
        for a in range(3)
    ]
    pair_list = ((0, 0), (1, 1), (2, 2), (0, 1), (0, 2), (1, 2))
    return [
        left_side[a][0] * rotation[b][0]
        + left_side[a][1] * rotation[b][1]
        + left_side[a][2] * rotation[b][2]
        for a, b in pair_list
    ]


def rotation_at(load):
    lane = lax.broadcasted_iota(jnp.int32, (BRICK, LANES), 1)
    matrix = []
    for a in range(3):
        here = load(a, 1)
        centre = here[1:BRICK + 1]
        along_z = (load(a, 2)[1:BRICK + 1] - load(a, 0)[1:BRICK + 1]) * 0.5
        along_y = (here[2:BRICK + 2] - here[0:BRICK]) * 0.5
        later = jnp.where(lane == LANES - 1, 0.0, pltpu.roll(centre, LANES - 1, 1))
        earlier = jnp.where(lane == 0, 0.0, pltpu.roll(centre, 1, 1))
        gradients = [along_z, along_y, (later - earlier) * 0.5]
        gradients[a] = gradients[a] + 1.0
        matrix.append(gradients)
    return polar_factor(matrix)


def warp_kernel(
    code_ref, slot_ref, brick_ref, u_ref, out_ref,
    asked, rows_ref, rows_half, crops, arrived,
    u_pad, u_rows, u_all, rotations, placed, fields,
    ask_send, ask_recv, crop_send, crop_recv, u_send, u_recv, up_send, up_recv,
    down_send, down_recv, field_send, field_recv,
):
    count, subjects = arrived.shape[0], fields.shape[0]
    chunk = arrived.shape[1]
    capacity = chunk // ROWS
    me_s, me_k = lax.axis_index("subj"), lax.axis_index("slab")
    barrier = pltpu.get_barrier_semaphore()
    has_before, has_after = me_k > 0, me_k < count - 1

    def peer_slab(t):
        turn = (t + 1) // 2
        return (me_k + count // 2 + turn * (1 - 2 * ((t + 1) % 2)) + count) % count

    def peer_subj(t):
        return (me_s + t) % subjects

    def greet(s, k):
        pl.semaphore_signal(barrier, inc=1, device_id=(s, k), device_id_type=MESH)

    def greet_slab(t, carry):
        greet(me_s, peer_slab(t))
        return carry

    lax.fori_loop(0, count - 1, greet_slab, 0)
    for t in range(1, subjects):
        greet(peer_subj(t), me_k)

    @pl.when(has_before)
    def _():
        for t in range(1, subjects):
            greet(peer_subj(t), me_k - 1)

    @pl.when(has_after)
    def _():
        for t in range(1, subjects):
            greet(peer_subj(t), me_k + 1)

    def remote(source, target, send, recv, s, k):
        return pltpu.make_async_remote_copy(
            src_ref=source, dst_ref=target, send_sem=send, recv_sem=recv,
            device_id=(s, k), device_id_type=MESH,
        )

    edge = jnp.zeros((8, LANES), jnp.float32)
    height = u_ref.shape[2]

    def pad_rows(at, carry):
        a, z = at // SLAB_Z, at % SLAB_Z
        u_pad[0:8, :] = edge
        u_pad[8:8 + height, :] = u_ref[a, z]
        u_pad[8 + height:16 + height, :] = edge
        for r in range(subjects):
            first = 7 + r * BRICK
            u_rows[r, a, z] = u_pad[first:first + BRICK + 2, :].astype(jnp.bfloat16)
        return carry

    lax.fori_loop(0, 3 * SLAB_Z, pad_rows, 0)

    neighbours = (me_k + count - 1) // count + (2 * count - 2 - me_k) // count
    pl.semaphore_wait(barrier, count - 1 + (subjects - 1) * (1 + neighbours))

    def ask(k):
        return remote(code_ref.at[k], asked.at[me_k], ask_send.at[k], ask_recv.at[me_k], me_s, k)

    def ask_from(k):
        return remote(code_ref.at[k], asked.at[k], ask_send.at[k], ask_recv.at[k], me_s, k)

    def start_ask(t, carry):
        ask(peer_slab(t)).start()
        return carry

    lax.fori_loop(0, count - 1, start_ask, 0)
    asked[me_k] = code_ref[me_k]

    def u_block(r):
        return remote(
            u_rows.at[r], u_all.at[me_s, :, pl.ds(1, SLAB_Z)], u_send.at[r], u_recv.at[me_s], r, me_k
        )

    def u_block_from(s):
        return remote(
            u_rows.at[s], u_all.at[s, :, pl.ds(1, SLAB_Z)], u_send.at[s], u_recv.at[s], s, me_k
        )

    def u_before(r, s):
        return remote(
            u_rows.at[r, :, pl.ds(0, 1)], u_all.at[s, :, pl.ds(SLAB_Z + 1, 1)],
            up_send.at[r], up_recv.at[s], r, me_k - 1,
        )

    def u_after(r, s):
        return remote(
            u_rows.at[r, :, pl.ds(SLAB_Z - 1, 1)], u_all.at[s, :, pl.ds(0, 1)],
            down_send.at[r], down_recv.at[s], r, me_k + 1,
        )

    for t in range(1, subjects):
        u_block(peer_subj(t)).start()

    @pl.when(has_before)
    def _():
        for t in range(subjects):
            u_before(peer_subj(t), me_s).start()

    @pl.when(has_after)
    def _():
        for t in range(subjects):
            u_after(peer_subj(t), me_s).start()

    def keep_u(at, carry):
        a, z = at // SLAB_Z, at % SLAB_Z
        u_all[me_s, a, z + 1] = u_rows[me_s, a, z]
        return carry

    lax.fori_loop(0, 3 * SLAB_Z, keep_u, 0)
    rim = jnp.zeros((BRICK + 2, LANES), jnp.bfloat16)

    @pl.when(me_k == 0)
    def _():
        for s in range(subjects):
            for a in range(3):
                u_all[s, a, 0] = rim

    @pl.when(me_k == count - 1)
    def _():
        for s in range(subjects):
            for a in range(3):
                u_all[s, a, SLAB_Z + 1] = rim

    relayout_bricks(brick_ref, rows_ref)
    for j in range(4):
        rows_half[:, j * LANES:(j + 1) * LANES] = rows_ref[j].astype(jnp.bfloat16)
    select = selection()

    def wait_ask(t, carry):
        ask_from(peer_slab(t)).wait_recv()
        return carry

    lax.fori_loop(0, count - 1, wait_ask, 0)
    def crop(k):
        return crop_rows(asked[k], capacity, rows_half[...], select).astype(jnp.bfloat16)

    def give(k):
        return remote(crops.at[k], arrived.at[me_k], crop_send.at[k], crop_recv.at[me_k], me_s, k)

    def take(k):
        return remote(crops.at[k], arrived.at[k], crop_send.at[k], crop_recv.at[k], me_s, k)

    def crop_and_give(t, carry):
        reader = peer_slab(t)
        crops[reader] = crop(reader)
        give(reader).start()
        return carry

    lax.fori_loop(0, count - 1, crop_and_give, 0)

    arrived[me_k] = crop(me_k)

    for t in range(1, subjects):
        u_block_from(peer_subj(t)).wait_recv()

    @pl.when(has_before)
    def _():
        for t in range(subjects):
            u_after(peer_subj(t), peer_subj(t)).wait_recv()

    @pl.when(has_after)
    def _():
        for t in range(subjects):
            u_before(peer_subj(t), peer_subj(t)).wait_recv()

    def rotate(at, carry):
        s, z = at // SLAB_Z, at % SLAB_Z
        rotation = rotation_at(lambda a, dz: u_all[s, a, z + dz].astype(jnp.float32))
        for a in range(3):
            for b in range(3):
                rotations[s, z, a * 3 + b] = rotation[a][b]
        return carry

    lax.fori_loop(0, subjects * SLAB_Z, rotate, 0)

    def collect(t, carry):
        take(peer_slab(t)).wait_recv()
        return carry

    lax.fori_loop(0, count - 1, collect, 0)

    def share(r):
        return remote(
            placed.at[r], fields.at[me_s], field_send.at[r], field_recv.at[me_s], r, me_k
        )

    def shared_from(s):
        return remote(placed.at[s], fields.at[s], field_send.at[s], field_recv.at[s], s, me_k)

    def place(row):
        halves = place_row(slot_ref, arrived, row)
        return jnp.concatenate(halves, axis=1).astype(jnp.bfloat16)

    def place_and_share(t, carry):
        r = peer_subj(t)
        placed[r] = place(r)
        share(r).start()
        return carry

    lax.fori_loop(1, subjects, place_and_share, 0)
    fields[me_s] = place(me_s)

    def add_subject(t, first):
        s = peer_subj(t)

        def step(z, carry):
            rotation = [[rotations[s, z, a * 3 + b] for b in range(3)] for a in range(3)]
            tensor = [
                fields[s, z * COMP + c].astype(jnp.float32) * (1.0 / subjects) for c in range(COMP)
            ]
            rotated = reorient(tensor, rotation)
            for c in range(COMP):
                out_ref[c, z] = rotated[c] if first else out_ref[c, z] + rotated[c]
            return carry

        lax.fori_loop(0, SLAB_Z, step, 0)

    add_subject(0, True)
    for t in range(1, subjects):
        shared_from(peer_subj(t)).wait_recv()
        add_subject(t, False)

    def finish(t, carry):
        k = peer_slab(t)
        ask(k).wait_send()
        give(k).wait_send()
        return carry

    lax.fori_loop(0, count - 1, finish, 0)
    for t in range(1, subjects):
        u_block(peer_subj(t)).wait_send()
        share(peer_subj(t)).wait_send()

    @pl.when(has_before)
    def _():
        for t in range(subjects):
            u_before(peer_subj(t), me_s).wait_send()

    @pl.when(has_after)
    def _():
        for t in range(subjects):
            u_after(peer_subj(t), me_s).wait_send()


MESH = pl.DeviceIdType.MESH
VMEM_SPEC = pl.BlockSpec(memory_space=pltpu.VMEM)
SMEM_SPEC = pl.BlockSpec(memory_space=pltpu.SMEM)


def slot_tables(brick_ids, brick_offsets, held, slab_count, capacity):
    wanted = brick_ids[0]
    pieces = wanted.shape[0]
    owner, local = wanted // held, wanted % held
    positions = jnp.arange(pieces, dtype=jnp.int32)
    earlier = (owner[:, None] == owner[None, :]) & (positions[None, :] < positions[:, None])
    slot_of = owner * capacity + jnp.sum(earlier.astype(jnp.int32), axis=1)
    start_z = brick_offsets[0, 0] + lax.axis_index("slab") % ZQ * SLAB_Z
    shift = brick_offsets[0, 1] * EDGE + brick_offsets[0, 2]
    code = (local * BRICK_ROWS + start_z * COMP) * LANES + shift
    hits = slot_of[:, None] == jnp.arange(slab_count * capacity, dtype=jnp.int32)[None, :]
    return slot_of, jnp.sum(jnp.where(hits, code[:, None], 0), axis=0)


def shards(source_bricks, brick_ids, brick_offsets, deformation):
    slab_count, subjects = lax.axis_size("slab"), lax.axis_size("subj")
    pieces = brick_ids.shape[1]
    held = source_bricks.shape[1]
    capacity = max(2, 3 * pieces // (2 * slab_count))
    chunk = capacity * ROWS
    slot_of, code = slot_tables(brick_ids, brick_offsets, held, slab_count, capacity)
    code = jnp.pad(code.reshape(slab_count, 1, capacity), ((0, 0), (0, 0), (0, LANES - capacity)))
    rim_rows = BRICK + 2
    bf16, f32, dma = jnp.bfloat16, jnp.float32, pltpu.SemaphoreType.DMA
    per_slab, per_subject = dma((slab_count,)), dma((subjects,))
    return pl.pallas_call(
        warp_kernel,
        out_shape=jax.ShapeDtypeStruct((COMP, SLAB_Z, BRICK, LANES), f32),
        in_specs=[VMEM_SPEC, SMEM_SPEC, VMEM_SPEC, VMEM_SPEC],
        out_specs=VMEM_SPEC,
        scratch_shapes=[
            pltpu.VMEM((slab_count, 1, LANES), jnp.int32),
            pltpu.VMEM((4, held * BRICK_ROWS, LANES), f32),
            pltpu.VMEM((held * BRICK_ROWS, 4 * LANES), bf16),
            pltpu.VMEM((slab_count, chunk, FLAT), bf16),
            pltpu.VMEM((slab_count, chunk, FLAT), bf16),
            pltpu.VMEM((deformation.shape[3] + 16, LANES), f32),
            pltpu.VMEM((subjects, 3, SLAB_Z, rim_rows, LANES), bf16),
            pltpu.VMEM((subjects, 3, SLAB_Z + 2, rim_rows, LANES), bf16),
            pltpu.VMEM((subjects, SLAB_Z, 9, BRICK, LANES), f32),
            pltpu.VMEM((subjects, ROWS, BRICK, LANES), bf16),
            pltpu.VMEM((subjects, ROWS, BRICK, LANES), bf16),
            per_slab, per_slab, per_slab, per_slab,
            per_subject, per_subject, per_subject, per_subject,
            per_subject, per_subject, per_subject, per_subject,
        ],
        compiler_params=pltpu.CompilerParams(
            vmem_limit_bytes=48 << 20, collective_id=0, has_side_effects=True
        ),
    )(code, slot_of, source_bricks[0], deformation[0])


def solution(mesh):
    in_specs = (
        P("subj", "slab", None),
        P("subj", "slab"),
        P("subj", None, "slab"),
        P("subj", None, "slab", None, None),
    )
    out_specs = P(None, "slab", "subj", None)
    return jax.shard_map(shards, mesh=mesh, in_specs=in_specs, out_specs=out_specs, check_vma=False)
```

time: 62.9 us -> 35.7 us (0.57)
  Pallas kernels: 9.3 us -> 31.6 us
  blocking collectives: 20.7 us -> 0 us
  waiting for transfers between devices: 16.9 us -> 0 us
  starting transfers between devices: 11 us -> 0 us
  other arithmetic: 1.88 us -> 0.3 us
  local copies, waits for them, and re-layouts: 2.65 us -> 3.57 us
    pallas_call x3 -> x1, Pallas kernels: 9.3 us -> 31.6 us  [shards(): pl.pallas_call(warp_kernel, out_shape=jax.ShapeDtypeStruct((COMP, SLAB_Z,...]
    all_to_all x2 -> x0, blocking collectives: 20.7 us -> none  [the longest x1 11.7 us: shards(): lax.all_to_all(code.reshape(slab_count, capacity), 'slab', split_axis=0,...]
    all_to_all x2 -> x0, waiting for transfers between devices: 14 us -> none  [the longest x1 9 us: shards(): lax.all_to_all(cropped, 'slab', split_axis=0, concat_axis=0, tiled=True)]
    all_to_all x2 -> x0, starting transfers between devices: 7.39 us -> none  [the longest x1 3.72 us: row_windows(): lax.all_to_all(blocks, 'subj', split_axis=0, concat_axis=0, tiled=True)]
    ppermute x2 -> x0, starting transfers between devices: 3.59 us -> none  [the longest x1 2.3 us: row_windows(): lax.ppermute(u[:, -1:], 'slab', [(i, i + 1) for i in range(count - 1)])]
    ppermute x2 -> x0, waiting for transfers between devices: 2.96 us -> none  [the longest x1 2.96 us: row_windows(): lax.ppermute(u[:, :1], 'slab', [(i + 1, i) for i in range(count - 1)])]
    unnamed x8 -> x9, local copies, waits for them, and re-layouts: 1.82 us -> 3.48 us
    another operation x1 -> x0, other arithmetic: 0.85 us -> none  [row_windows(): jnp.stack([u[:, :, r * BRICK:r * BRICK + BRICK + 2] for r in range(subjec...]
  transfers between devices with their start and end apart: 4 -> 0, of which waited for: 3 -> 0; matrix products, arithmetic and copies ran while one was open for 2% -> 0% of each run, Pallas kernels for 3% -> 0%
where the time goes in v2:
time: 35.7 us; the launch traced here: 35.5 us
  Pallas kernels  31.6 us (89%)
  local copies, waits for them, and re-layouts  3.57 us (10%)
    pallas_call x1, Pallas kernels, shards(): pl.pallas_call(warp_kernel, out_shape=jax.ShapeDtypeStruct((COMP, SLAB_Z,...  31.6 us
    unnamed x9, local copies, waits for them, and re-layouts  3.48 us

profile of v2, /device:TPU:0, one launch (start us, length us, event | category | flops | bytes accessed | tf_op | source)
XLA Modules:
  0.0 35.5 jit_solution(1490029208700519648)
XLA Ops:
  0.0 0.0 copy-start.3
  0.0 0.0 copy-start.2
  0.0 0.7 %copy-done.3 = s32[1,32]{1,0:T(1,128)S(1)} copy-done((s32[1,32]{1,0:T(1,128)S(1)}, s32[1,32]{1,0:T(1,128)}, u32[]{:S(2)}) %copy-start.3) | copy-done | bytes 152
  0.7 0.0 copy-done.2
  0.7 0.2 convert_reduce_fusion
  0.9 0.1 select_reduce_fusion
  1.0 0.1 reshape.92
  1.1 0.0 copy-start
  1.1 1.1 %copy-done = bf16[1,8,48000]{2,1,0:T(8,128)(2,1)S(1)} copy-done((bf16[1,8,48000]{2,1,0:T(8,128)(2,1)S(1)}, bf16[1,8,48000]{2,1,0:T(8,128)(2,1)}, u32[]{:S(2)}) %copy-start) | copy-done | bytes 768024
  2.2 0.0 copy-start.1
  2.2 1.0 %copy-done.1 = f32[1,3,4,64,128]{4,3,2,1,0:T(8,128)S(1)} copy-done((f32[1,3,4,64,128]{4,3,2,1,0:T(8,128)S(1)}, f32[1,3,4,64,128]{4,3,2,1,0:T(8,128)}, u32[]{:S(2)}) %copy-start.1) | copy-done | bytes 393240
  3.2 31.6 %shard_map.46 = f32[6,4,16,128]{3,2,1,0:T(8,128)S(1)} custom-call(s32[8,1,128]{2,1,0:T(1,128)S(1)} %pad.4.code_ref, s32[32]{0:T(128)S(1)} %multiply_add_fusion.slot_ref, bf16[8,48000]{1,0:T(8,128)(2,1)S(1)} %bitcast.26, f32[3,4,64,128]{3,2,1,0:T(8,128)S(1)} %bitcast.27), custom_call_target="tpu_custom_call" | custom-call | tf_op jit(solution)/shard_map/pallas_call | solution.py:454
  34.8 0.7 %copy.9 = f32[6,4,16,128]{3,2,1,0:T(8,128)} copy(f32[6,4,16,128]{3,2,1,0:T(8,128)S(1)} %shard_map.46) | data formatting | bytes 393216
  (4 shorter events, 0.0 us)
Async XLA Ops:
  0.0 0.7 %copy-start.3 = (s32[1,32]{1,0:T(1,128)S(1)}, s32[1,32]{1,0:T(1,128)}, u32[]{:S(2)}) copy-start(s32[1,32]{1,0:T(1,128)} %param.5) | copy-start | bytes 388
  0.0 0.7 %copy-start.2 = (s32[1,3,32]{2,0,1:T(1,128)S(1)}, s32[1,3,32]{2,0,1:T(1,128)}, u32[]{:S(2)}) copy-start(s32[1,3,32]{2,0,1:T(1,128)} %param.6) | copy-start | bytes 1156
  1.1 1.1 %copy-start = (bf16[1,8,48000]{2,1,0:T(8,128)(2,1)S(1)}, bf16[1,8,48000]{2,1,0:T(8,128)(2,1)}, u32[]{:S(2)}) copy-start(bf16[1,8,48000]{2,1,0:T(8,128)(2,1)} %param.4) | copy-start | bytes 2304004
  2.2 1.0 %copy-start.1 = (f32[1,3,4,64,128]{4,3,2,1,0:T(8,128)S(1)}, f32[1,3,4,64,128]{4,3,2,1,0:T(8,128)}, u32[]{:S(2)}) copy-start(f32[1,3,4,64,128]{4,3,2,1,0:T(8,128)} %param.7) | copy-start | bytes 1179652

commit v3 on v2

--- a/solution.py
+++ b/solution.py
@@ -15,6 +15,8 @@
 LANES = 128
 ROWS = COMP * SLAB_Z
 BRICK_ROWS = COMP * EDGE
+PARTS = COMP // 2
+PART_ROWS = 2 * SLAB_Z
 SPAN = 384
 FLAT = BRICK * BRICK
 
@@ -52,16 +54,19 @@
 
 def crop_rows(codes, capacity, rows, select):
     depth = rows.shape[0]
-    row = lax.broadcasted_iota(jnp.int32, (ROWS, depth), 0)
-    column = lax.broadcasted_iota(jnp.int32, (ROWS, depth), 1)
+    row = lax.broadcasted_iota(jnp.int32, (PART_ROWS, depth), 0)
+    offset = lax.broadcasted_iota(jnp.int32, (PART_ROWS, depth), 1) - (row // 2 * COMP + row % 2)
     hits, shifts = [], []
     for slot in range(capacity):
         code = codes[:, slot:slot + 1]
         start = lax.shift_right_logical(code, jnp.full(code.shape, 7, jnp.int32))
-        hits.append((column - row == jnp.broadcast_to(start, (ROWS, depth))).astype(jnp.float32))
-        shifts.append(jnp.broadcast_to(code & (LANES - 1), (ROWS, LANES)))
-    hit = jnp.concatenate(hits, axis=0).astype(jnp.bfloat16)
-    shift = jnp.concatenate(shifts, axis=0)
+        hits.append(offset - jnp.broadcast_to(start, (PART_ROWS, depth)))
+        shifts.append(jnp.broadcast_to(code & (LANES - 1), (PART_ROWS, LANES)))
+    hit = jnp.concatenate(
+        [(hits[slot] == 2 * part).astype(jnp.float32) for part in range(PARTS) for slot in range(capacity)],
+        axis=0,
+    ).astype(jnp.bfloat16)
+    shift = jnp.concatenate(shifts * PARTS, axis=0)
     found = jnp.dot(hit, rows, preferred_element_type=jnp.float32)
     tiles = [found[:, j * LANES:(j + 1) * LANES] for j in range(4)]
     for bit in (1, 2, 4, 8, 16, 32, 64):
@@ -87,21 +92,25 @@
     return value
 
 
-def place_row(slot_ref, arrived, row):
+def placing_hits(slot_ref, row, depth):
     across = LANES // BRICK
-    depth = arrived.shape[0] * arrived.shape[1]
-    sub = lax.broadcasted_iota(jnp.int32, (8, depth), 0)
-    base = jnp.zeros((8, depth), jnp.int32)
+    sub = lax.broadcasted_iota(jnp.int32, (across, depth), 0)
+    base = jnp.zeros((across, depth), jnp.int32)
     for j in range(across):
-        base = jnp.where(sub == j, slot_ref[row * across + j] * ROWS, base)
-    offset = lax.broadcasted_iota(jnp.int32, (8, depth), 1) - base
-    hit = jnp.concatenate([(offset == n).astype(jnp.float32) for n in range(ROWS)], axis=0)
-    pieces = jnp.dot(
-        hit.astype(jnp.bfloat16), arrived[...].reshape(depth, FLAT), preferred_element_type=jnp.float32
-    )
-    return [
-        swap_groups(pieces[:, h * LANES:(h + 1) * LANES].reshape(ROWS, 8, LANES)) for h in range(2)
+        base = jnp.where(sub == j, slot_ref[row * across + j] * PART_ROWS, base)
+    offset = lax.broadcasted_iota(jnp.int32, (across, depth), 1) - base
+    return jnp.concatenate(
+        [(offset == n).astype(jnp.float32) for n in range(PART_ROWS)], axis=0
+    ).astype(jnp.bfloat16)
+
+
+def place_row(hit, windows):
+    pieces = jnp.dot(hit, windows, preferred_element_type=jnp.float32)
+    halves = [
+        swap_groups(pieces[:, h * LANES:(h + 1) * LANES].reshape(PART_ROWS, 8, LANES))
+        for h in range(2)
     ]
+    return jnp.concatenate(halves, axis=1).astype(jnp.bfloat16)
 
 
 def polar_factor(matrix):
@@ -150,16 +159,15 @@
     ]
 
 
-def rotation_at(load):
+def rotation_at(centre, before, after):
     lane = lax.broadcasted_iota(jnp.int32, (BRICK, LANES), 1)
     matrix = []
     for a in range(3):
-        here = load(a, 1)
-        centre = here[1:BRICK + 1]
-        along_z = (load(a, 2)[1:BRICK + 1] - load(a, 0)[1:BRICK + 1]) * 0.5
-        along_y = (here[2:BRICK + 2] - here[0:BRICK]) * 0.5
-        later = jnp.where(lane == LANES - 1, 0.0, pltpu.roll(centre, LANES - 1, 1))
-        earlier = jnp.where(lane == 0, 0.0, pltpu.roll(centre, 1, 1))
+        here = centre[a][1:BRICK + 1]
+        along_z = (after[a] - before[a]) * 0.5
+        along_y = (centre[a][2:BRICK + 2] - centre[a][0:BRICK]) * 0.5
+        later = jnp.where(lane == LANES - 1, 0.0, pltpu.roll(here, LANES - 1, 1))
+        earlier = jnp.where(lane == 0, 0.0, pltpu.roll(here, 1, 1))
         gradients = [along_z, along_y, (later - earlier) * 0.5]
         gradients[a] = gradients[a] + 1.0
         matrix.append(gradients)
@@ -167,15 +175,18 @@
 
 
 def warp_kernel(
-    code_ref, slot_ref, brick_ref, u_ref, out_ref,
-    asked, rows_ref, rows_half, crops, arrived,
-    u_pad, u_rows, u_all, rotations, placed, fields,
+    code_ref, slot_ref, brick_hbm, u_hbm, out_ref,
+    brick_ref, u_ref, asked, rows_ref, rows_half, crops, arrived, hits,
+    u_pad, u_rows, u_edge, u_all, u_rim, rotations, placed, fields, load_sem,
     ask_send, ask_recv, crop_send, crop_recv, u_send, u_recv, up_send, up_recv,
     down_send, down_recv, field_send, field_recv,
 ):
-    count, subjects = arrived.shape[0], fields.shape[0]
-    chunk = arrived.shape[1]
-    capacity = chunk // ROWS
+    count, subjects = arrived.shape[1], fields.shape[0]
+    capacity = arrived.shape[2] // PART_ROWS
+    load_u = pltpu.make_async_copy(u_hbm.at[0], u_ref, load_sem.at[0])
+    load_u.start()
+    load_bricks = pltpu.make_async_copy(brick_hbm.at[0], brick_ref, load_sem.at[1])
+    load_bricks.start()
     me_s, me_k = lax.axis_index("subj"), lax.axis_index("slab")
     barrier = pltpu.get_barrier_semaphore()
     has_before, has_after = me_k > 0, me_k < count - 1
@@ -216,18 +227,25 @@
 
     edge = jnp.zeros((8, LANES), jnp.float32)
     height = u_ref.shape[2]
+    u_pad[0:8, :] = edge
+    u_pad[8 + height:16 + height, :] = edge
+    load_u.wait()
 
     def pad_rows(at, carry):
         a, z = at // SLAB_Z, at % SLAB_Z
-        u_pad[0:8, :] = edge
         u_pad[8:8 + height, :] = u_ref[a, z]
-        u_pad[8 + height:16 + height, :] = edge
         for r in range(subjects):
             first = 7 + r * BRICK
             u_rows[r, a, z] = u_pad[first:first + BRICK + 2, :].astype(jnp.bfloat16)
         return carry
 
     lax.fori_loop(0, 3 * SLAB_Z, pad_rows, 0)
+    for side in range(2):
+        for a in range(3):
+            for r in range(subjects):
+                u_edge[side, r, a] = u_ref[
+                    a, side * (SLAB_Z - 1), r * BRICK:(r + 1) * BRICK, :
+                ].astype(jnp.bfloat16)
 
     neighbours = (me_k + count - 1) // count + (2 * count - 2 - me_k) // count
     pl.semaphore_wait(barrier, count - 1 + (subjects - 1) * (1 + neighbours))
@@ -246,25 +264,19 @@
     asked[me_k] = code_ref[me_k]
 
     def u_block(r):
-        return remote(
-            u_rows.at[r], u_all.at[me_s, :, pl.ds(1, SLAB_Z)], u_send.at[r], u_recv.at[me_s], r, me_k
-        )
+        return remote(u_rows.at[r], u_all.at[me_s], u_send.at[r], u_recv.at[me_s], r, me_k)
 
     def u_block_from(s):
-        return remote(
-            u_rows.at[s], u_all.at[s, :, pl.ds(1, SLAB_Z)], u_send.at[s], u_recv.at[s], s, me_k
-        )
+        return remote(u_rows.at[s], u_all.at[s], u_send.at[s], u_recv.at[s], s, me_k)
 
     def u_before(r, s):
         return remote(
-            u_rows.at[r, :, pl.ds(0, 1)], u_all.at[s, :, pl.ds(SLAB_Z + 1, 1)],
-            up_send.at[r], up_recv.at[s], r, me_k - 1,
+            u_edge.at[0, r], u_rim.at[s, 1], up_send.at[r], up_recv.at[s], r, me_k - 1
         )
 
     def u_after(r, s):
         return remote(
-            u_rows.at[r, :, pl.ds(SLAB_Z - 1, 1)], u_all.at[s, :, pl.ds(0, 1)],
-            down_send.at[r], down_recv.at[s], r, me_k + 1,
+            u_edge.at[1, r], u_rim.at[s, 0], down_send.at[r], down_recv.at[s], r, me_k + 1
         )
 
     for t in range(1, subjects):
@@ -282,24 +294,25 @@
 
     def keep_u(at, carry):
         a, z = at // SLAB_Z, at % SLAB_Z
-        u_all[me_s, a, z + 1] = u_rows[me_s, a, z]
+        u_all[me_s, a, z] = u_rows[me_s, a, z]
         return carry
 
     lax.fori_loop(0, 3 * SLAB_Z, keep_u, 0)
-    rim = jnp.zeros((BRICK + 2, LANES), jnp.bfloat16)
+    rim = jnp.zeros((BRICK, LANES), jnp.bfloat16)
 
     @pl.when(me_k == 0)
     def _():
         for s in range(subjects):
             for a in range(3):
-                u_all[s, a, 0] = rim
+                u_rim[s, 0, a] = rim
 
     @pl.when(me_k == count - 1)
     def _():
         for s in range(subjects):
             for a in range(3):
-                u_all[s, a, SLAB_Z + 1] = rim
-
+                u_rim[s, 1, a] = rim
+
+    load_bricks.wait()
     relayout_bricks(brick_ref, rows_ref)
     for j in range(4):
         rows_half[:, j * LANES:(j + 1) * LANES] = rows_ref[j].astype(jnp.bfloat16)
@@ -310,24 +323,46 @@
         return carry
 
     lax.fori_loop(0, count - 1, wait_ask, 0)
-    def crop(k):
-        return crop_rows(asked[k], capacity, rows_half[...], select).astype(jnp.bfloat16)
-
-    def give(k):
-        return remote(crops.at[k], arrived.at[me_k], crop_send.at[k], crop_recv.at[me_k], me_s, k)
-
-    def take(k):
-        return remote(crops.at[k], arrived.at[k], crop_send.at[k], crop_recv.at[k], me_s, k)
+    def crop(k, target):
+        value = crop_rows(asked[k], capacity, rows_half[...], select).astype(jnp.bfloat16)
+        for part in range(PARTS):
+            target[part, k] = value[part * capacity * PART_ROWS:(part + 1) * capacity * PART_ROWS]
+
+    def give(k, part):
+        return remote(
+            crops.at[part, k], arrived.at[part, me_k],
+            crop_send.at[part, k], crop_recv.at[part, me_k], me_s, k,
+        )
+
+    def take(k, part):
+        return remote(
+            crops.at[part, k], arrived.at[part, k],
+            crop_send.at[part, k], crop_recv.at[part, k], me_s, k,
+        )
 
     def crop_and_give(t, carry):
         reader = peer_slab(t)
-        crops[reader] = crop(reader)
-        give(reader).start()
+        crop(reader, crops)
+        give(reader, 0).start()
         return carry
 
     lax.fori_loop(0, count - 1, crop_and_give, 0)
 
-    arrived[me_k] = crop(me_k)
+    for part in range(1, PARTS):
+        def give_part(t, carry):
+            give(peer_slab(t), part).start()
+            return carry
+
+        lax.fori_loop(0, count - 1, give_part, 0)
+
+    crop(me_k, arrived)
+    depth = count * capacity * PART_ROWS
+
+    def make_hits(row, carry):
+        hits[row] = placing_hits(slot_ref, row, depth)
+        return carry
+
+    lax.fori_loop(0, subjects, make_hits, 0)
 
     for t in range(1, subjects):
         u_block_from(peer_subj(t)).wait_recv()
@@ -342,42 +377,53 @@
         for t in range(subjects):
             u_before(peer_subj(t), peer_subj(t)).wait_recv()
 
-    def rotate(at, carry):
-        s, z = at // SLAB_Z, at % SLAB_Z
-        rotation = rotation_at(lambda a, dz: u_all[s, a, z + dz].astype(jnp.float32))
-        for a in range(3):
-            for b in range(3):
-                rotations[s, z, a * 3 + b] = rotation[a][b]
-        return carry
-
-    lax.fori_loop(0, subjects * SLAB_Z, rotate, 0)
-
-    def collect(t, carry):
-        take(peer_slab(t)).wait_recv()
-        return carry
-
-    lax.fori_loop(0, count - 1, collect, 0)
-
-    def share(r):
+    def rotate(s, carry):
+        for z in range(SLAB_Z):
+            layers = [
+                [u_all[s, a, near].astype(jnp.float32) if 0 <= near < SLAB_Z else None for a in range(3)]
+                for near in (z - 1, z, z + 1)
+            ]
+            beside = [
+                [
+                    u_rim[s, side, a].astype(jnp.float32)
+                    if layers[2 * side][a] is None
+                    else layers[2 * side][a][1:BRICK + 1]
+                    for a in range(3)
+                ]
+                for side in range(2)
+            ]
+            rotation = rotation_at(layers[1], beside[0], beside[1])
+            for a in range(3):
+                for b in range(3):
+                    rotations[s, z, a * 3 + b] = rotation[a][b]
+        return carry
+
+    lax.fori_loop(0, subjects, rotate, 0)
+
+    def share(r, part):
         return remote(
-            placed.at[r], fields.at[me_s], field_send.at[r], field_recv.at[me_s], r, me_k
-        )
-
-    def shared_from(s):
-        return remote(placed.at[s], fields.at[s], field_send.at[s], field_recv.at[s], s, me_k)
-
-    def place(row):
-        halves = place_row(slot_ref, arrived, row)
-        return jnp.concatenate(halves, axis=1).astype(jnp.bfloat16)
-
-    def place_and_share(t, carry):
-        r = peer_subj(t)
-        placed[r] = place(r)
-        share(r).start()
-        return carry
-
-    lax.fori_loop(1, subjects, place_and_share, 0)
-    fields[me_s] = place(me_s)
+            placed.at[r, part], fields.at[me_s, part],
+            field_send.at[part, r], field_recv.at[part, me_s], r, me_k,
+        )
+
+    def shared_from(s, part):
+        return remote(
+            placed.at[s, part], fields.at[s, part],
+            field_send.at[part, s], field_recv.at[part, s], s, me_k,
+        )
+
+    for part in range(PARTS):
+        def collect(t, carry):
+            take(peer_slab(t), part).wait_recv()
+            return carry
+
+        lax.fori_loop(0, count - 1, collect, 0)
+        windows = arrived[part].reshape(depth, FLAT)
+        for t in range(1, subjects):
+            r = peer_subj(t)
+            placed[r, part] = place_row(hits[r], windows)
+            share(r, part).start()
+        fields[me_s, part] = place_row(hits[me_s], windows)
 
     def add_subject(t, first):
         s = peer_subj(t)
@@ -385,7 +431,8 @@
         def step(z, carry):
             rotation = [[rotations[s, z, a * 3 + b] for b in range(3)] for a in range(3)]
             tensor = [
-                fields[s, z * COMP + c].astype(jnp.float32) * (1.0 / subjects) for c in range(COMP)
+                fields[s, c // 2, z * 2 + c % 2].astype(jnp.float32) * (1.0 / subjects)
+                for c in range(COMP)
             ]
             rotated = reorient(tensor, rotation)
             for c in range(COMP):
@@ -396,19 +443,22 @@
 
     add_subject(0, True)
     for t in range(1, subjects):
-        shared_from(peer_subj(t)).wait_recv()
+        for part in range(PARTS):
+            shared_from(peer_subj(t), part).wait_recv()
         add_subject(t, False)
 
     def finish(t, carry):
         k = peer_slab(t)
         ask(k).wait_send()
-        give(k).wait_send()
+        for part in range(PARTS):
+            give(k, part).wait_send()
         return carry
 
     lax.fori_loop(0, count - 1, finish, 0)
     for t in range(1, subjects):
         u_block(peer_subj(t)).wait_send()
-        share(peer_subj(t)).wait_send()
+        for part in range(PARTS):
+            share(peer_subj(t), part).wait_send()
 
     @pl.when(has_before)
     def _():
@@ -423,6 +473,7 @@
 
 MESH = pl.DeviceIdType.MESH
 VMEM_SPEC = pl.BlockSpec(memory_space=pltpu.VMEM)
+HBM_SPEC = pl.BlockSpec(memory_space=pl.ANY)
 SMEM_SPEC = pl.BlockSpec(memory_space=pltpu.SMEM)
 
 
@@ -445,37 +496,42 @@
     pieces = brick_ids.shape[1]
     held = source_bricks.shape[1]
     capacity = max(2, 3 * pieces // (2 * slab_count))
-    chunk = capacity * ROWS
+    part_rows = capacity * PART_ROWS
     slot_of, code = slot_tables(brick_ids, brick_offsets, held, slab_count, capacity)
     code = jnp.pad(code.reshape(slab_count, 1, capacity), ((0, 0), (0, 0), (0, LANES - capacity)))
-    rim_rows = BRICK + 2
     bf16, f32, dma = jnp.bfloat16, jnp.float32, pltpu.SemaphoreType.DMA
     per_slab, per_subject = dma((slab_count,)), dma((subjects,))
     return pl.pallas_call(
         warp_kernel,
         out_shape=jax.ShapeDtypeStruct((COMP, SLAB_Z, BRICK, LANES), f32),
-        in_specs=[VMEM_SPEC, SMEM_SPEC, VMEM_SPEC, VMEM_SPEC],
+        in_specs=[VMEM_SPEC, SMEM_SPEC, HBM_SPEC, HBM_SPEC],
         out_specs=VMEM_SPEC,
         scratch_shapes=[
+            pltpu.VMEM(source_bricks.shape[1:], bf16),
+            pltpu.VMEM(deformation.shape[1:], f32),
             pltpu.VMEM((slab_count, 1, LANES), jnp.int32),
             pltpu.VMEM((4, held * BRICK_ROWS, LANES), f32),
             pltpu.VMEM((held * BRICK_ROWS, 4 * LANES), bf16),
-            pltpu.VMEM((slab_count, chunk, FLAT), bf16),
-            pltpu.VMEM((slab_count, chunk, FLAT), bf16),
+            pltpu.VMEM((PARTS, slab_count, part_rows, FLAT), bf16),
+            pltpu.VMEM((PARTS, slab_count, part_rows, FLAT), bf16),
+            pltpu.VMEM((subjects, LANES // BRICK * PART_ROWS, slab_count * part_rows), bf16),
             pltpu.VMEM((deformation.shape[3] + 16, LANES), f32),
-            pltpu.VMEM((subjects, 3, SLAB_Z, rim_rows, LANES), bf16),
-            pltpu.VMEM((subjects, 3, SLAB_Z + 2, rim_rows, LANES), bf16),
+            pltpu.VMEM((subjects, 3, SLAB_Z, BRICK + 2, LANES), bf16),
+            pltpu.VMEM((2, subjects, 3, BRICK, LANES), bf16),
+            pltpu.VMEM((subjects, 3, SLAB_Z, BRICK + 2, LANES), bf16),
+            pltpu.VMEM((subjects, 2, 3, BRICK, LANES), bf16),
             pltpu.VMEM((subjects, SLAB_Z, 9, BRICK, LANES), f32),
-            pltpu.VMEM((subjects, ROWS, BRICK, LANES), bf16),
-            pltpu.VMEM((subjects, ROWS, BRICK, LANES), bf16),
-            per_slab, per_slab, per_slab, per_slab,
+            pltpu.VMEM((subjects, PARTS, PART_ROWS, BRICK, LANES), bf16),
+            pltpu.VMEM((subjects, PARTS, PART_ROWS, BRICK, LANES), bf16),
+            dma((2,)),
+            per_slab, per_slab, dma((PARTS, slab_count)), dma((PARTS, slab_count)),
             per_subject, per_subject, per_subject, per_subject,
-            per_subject, per_subject, per_subject, per_subject,
+            per_subject, per_subject, dma((PARTS, subjects)), dma((PARTS, subjects)),
         ],
         compiler_params=pltpu.CompilerParams(
             vmem_limit_bytes=48 << 20, collective_id=0, has_side_effects=True
         ),
-    )(code, slot_of, source_bricks[0], deformation[0])
+    )(code, slot_of, source_bricks, deformation)
 
 
 def solution(mesh):

time: 35.7 us -> 37.9 us (1.062)
  Pallas kernels: 31.6 us -> 33.8 us
    pallas_call x1, Pallas kernels: 31.6 us -> 33.8 us  [shards(): pl.pallas_call(warp_kernel, out_shape=jax.ShapeDtypeStruct((COMP, SLAB_Z,...]
where the time goes in v3:
time: 37.9 us; the launch traced here: 37.7 us
  Pallas kernels  33.8 us (89%)
  local copies, waits for them, and re-layouts  3.57 us (9%)
    pallas_call x1, Pallas kernels, shards(): pl.pallas_call(warp_kernel, out_shape=jax.ShapeDtypeStruct((COMP, SLAB_Z,...  33.8 us
    unnamed x9, local copies, waits for them, and re-layouts  3.48 us

profile of v3, /device:TPU:0, one launch (start us, length us, event | category | flops | bytes accessed | tf_op | source)
XLA Modules:
  0.0 37.7 jit_solution(17210441940910306786)
XLA Ops:
  0.0 0.0 copy-start.3
  0.0 0.0 copy-start.2
  0.0 0.7 %copy-done.3 = s32[1,32]{1,0:T(1,128)S(1)} copy-done((s32[1,32]{1,0:T(1,128)S(1)}, s32[1,32]{1,0:T(1,128)}, u32[]{:S(2)}) %copy-start.3) | copy-done | bytes 152
  0.7 0.0 copy-done.2
  0.7 0.2 convert_reduce_fusion
  0.9 0.1 select_reduce_fusion
  1.0 0.1 reshape.92
  1.1 0.0 copy-start
  1.1 1.1 %copy-done = bf16[1,8,48000]{2,1,0:T(8,128)(2,1)S(1)} copy-done((bf16[1,8,48000]{2,1,0:T(8,128)(2,1)S(1)}, bf16[1,8,48000]{2,1,0:T(8,128)(2,1)}, u32[]{:S(2)}) %copy-start) | copy-done | bytes 768024
  2.2 0.0 copy-start.1
  2.2 1.0 %copy-done.1 = f32[1,3,4,64,128]{4,3,2,1,0:T(8,128)S(1)} copy-done((f32[1,3,4,64,128]{4,3,2,1,0:T(8,128)S(1)}, f32[1,3,4,64,128]{4,3,2,1,0:T(8,128)}, u32[]{:S(2)}) %copy-start.1) | copy-done | bytes 393240
  3.2 33.8 %shard_map.46 = f32[6,4,16,128]{3,2,1,0:T(8,128)S(1)} custom-call(s32[8,1,128]{2,1,0:T(1,128)S(1)} %pad.4.code_ref, s32[32]{0:T(128)S(1)} %multiply_add_fusion.slot_ref, bf16[1,8,48000]{2,1,0:T(8,128)(2,1)S(1)} %copy-done, f32[1,3,4,64,128]{4,3,2,1,0:T(8,128)S(1)} %copy-done.1), custom_call_target="tpu_custom_call" | custom-call | tf_op jit(solution)/shard_map/pallas_call | solution.py:504
  37.0 0.7 %copy.9 = f32[6,4,16,128]{3,2,1,0:T(8,128)} copy(f32[6,4,16,128]{3,2,1,0:T(8,128)S(1)} %shard_map.46) | data formatting | bytes 393216
  (4 shorter events, 0.0 us)
Async XLA Ops:
  0.0 0.7 %copy-start.3 = (s32[1,32]{1,0:T(1,128)S(1)}, s32[1,32]{1,0:T(1,128)}, u32[]{:S(2)}) copy-start(s32[1,32]{1,0:T(1,128)} %param.5) | copy-start | bytes 388
  0.0 0.7 %copy-start.2 = (s32[1,3,32]{2,0,1:T(1,128)S(1)}, s32[1,3,32]{2,0,1:T(1,128)}, u32[]{:S(2)}) copy-start(s32[1,3,32]{2,0,1:T(1,128)} %param.6) | copy-start | bytes 1156
  1.1 1.1 %copy-start = (bf16[1,8,48000]{2,1,0:T(8,128)(2,1)S(1)}, bf16[1,8,48000]{2,1,0:T(8,128)(2,1)}, u32[]{:S(2)}) copy-start(bf16[1,8,48000]{2,1,0:T(8,128)(2,1)} %brick_hbm.1) | copy-start | bytes 2304004
  2.2 1.0 %copy-start.1 = (f32[1,3,4,64,128]{4,3,2,1,0:T(8,128)S(1)}, f32[1,3,4,64,128]{4,3,2,1,0:T(8,128)}, u32[]{:S(2)}) copy-start(f32[1,3,4,64,128]{4,3,2,1,0:T(8,128)} %u_hbm.1) | copy-start | bytes 1179652

commit v4 on v3

--- a/solution.py
+++ b/solution.py
@@ -29,7 +29,7 @@
     def step(group, carry):
         for m in range(8):
             cz = group * 8 + m
-            row = cz % EDGE * COMP + cz // EDGE
+            row = cz % EDGE * (held * COMP) + cz // EDGE
             shift = 16 * m
             tiles = []
             for j in range(4):
@@ -40,7 +40,7 @@
                 value = tiles[j]
                 if shift and j < 3:
                     value = jnp.where(lane < LANES - shift, tiles[j], tiles[j + 1])
-                rows_ref[j, pl.ds(row, held, stride=BRICK_ROWS), :] = value
+                rows_ref[j, pl.ds(row, held, stride=COMP), :] = value
         return carry
 
     lax.fori_loop(0, BRICK_ROWS // 8, step, 0)
@@ -54,8 +54,9 @@
 
 def crop_rows(codes, capacity, rows, select):
     depth = rows.shape[0]
+    layer = depth // (SLAB_Z + 2 * PAD)
     row = lax.broadcasted_iota(jnp.int32, (PART_ROWS, depth), 0)
-    offset = lax.broadcasted_iota(jnp.int32, (PART_ROWS, depth), 1) - (row // 2 * COMP + row % 2)
+    offset = lax.broadcasted_iota(jnp.int32, (PART_ROWS, depth), 1) - (row // 2 * layer + row % 2)
     hits, shifts = [], []
     for slot in range(capacity):
         code = codes[:, slot:slot + 1]
@@ -323,8 +324,12 @@
         return carry
 
     lax.fori_loop(0, count - 1, wait_ask, 0)
+    layer = brick_ref.shape[0] * COMP
+
     def crop(k, target):
-        value = crop_rows(asked[k], capacity, rows_half[...], select).astype(jnp.bfloat16)
+        first = pl.multiple_of(k % ZQ * SLAB_Z * layer, 16)
+        rows = rows_half[pl.ds(first, (SLAB_Z + 2 * PAD) * layer), :]
+        value = crop_rows(asked[k], capacity, rows, select).astype(jnp.bfloat16)
         for part in range(PARTS):
             target[part, k] = value[part * capacity * PART_ROWS:(part + 1) * capacity * PART_ROWS]
 
@@ -473,7 +478,7 @@
 
 MESH = pl.DeviceIdType.MESH
 VMEM_SPEC = pl.BlockSpec(memory_space=pltpu.VMEM)
-HBM_SPEC = pl.BlockSpec(memory_space=pl.ANY)
+HBM_SPEC = pl.BlockSpec(memory_space=pltpu.HBM)
 SMEM_SPEC = pl.BlockSpec(memory_space=pltpu.SMEM)
 
 
@@ -484,9 +489,8 @@
     positions = jnp.arange(pieces, dtype=jnp.int32)
     earlier = (owner[:, None] == owner[None, :]) & (positions[None, :] < positions[:, None])
     slot_of = owner * capacity + jnp.sum(earlier.astype(jnp.int32), axis=1)
-    start_z = brick_offsets[0, 0] + lax.axis_index("slab") % ZQ * SLAB_Z
     shift = brick_offsets[0, 1] * EDGE + brick_offsets[0, 2]
-    code = (local * BRICK_ROWS + start_z * COMP) * LANES + shift
+    code = (local + brick_offsets[0, 0] * held) * COMP * LANES + shift
     hits = slot_of[:, None] == jnp.arange(slab_count * capacity, dtype=jnp.int32)[None, :]
     return slot_of, jnp.sum(jnp.where(hits, code[:, None], 0), axis=0)
 

time: 37.9 us -> 37.9 us (level)
  other arithmetic: 0.3 us -> 1.63 us
  Pallas kernels: 33.8 us -> 33.1 us
  local copies, waits for them, and re-layouts: 3.57 us -> 2.89 us
    unnamed x9 -> x7, local copies, waits for them, and re-layouts: 3.48 us -> 2.8 us
    eq x1, other arithmetic: 0.01 us -> 0.68 us  [slot_tables(): owner[:, None] == owner[None, :]]
    pallas_call x1, Pallas kernels: 33.8 us -> 33.1 us  [shards(): pl.pallas_call(warp_kernel, out_shape=jax.ShapeDtypeStruct((COMP, SLAB_Z,...]
    select_n x1, other arithmetic: 0.01 us -> 0.67 us  [slot_tables(): owner, local = (wanted // held, wanted % held)]
where the time goes in v4:
time: 37.9 us; the launch traced here: 37.7 us
  Pallas kernels  33.1 us (87%)
  local copies, waits for them, and re-layouts  2.89 us (8%)
  other arithmetic  1.63 us (4%)
    pallas_call x1, Pallas kernels, shards(): pl.pallas_call(warp_kernel, out_shape=jax.ShapeDtypeStruct((COMP, SLAB_Z,...  33.1 us
    unnamed x7, local copies, waits for them, and re-layouts  2.8 us

profile of v4, /device:TPU:0, one launch (start us, length us, event | category | flops | bytes accessed | tf_op | source)
XLA Modules:
  0.0 37.7 jit_solution(11584291122038720646)
XLA Ops:
  0.0 0.0 copy-start.2
  0.0 0.7 %fusion.2 = s32[32]{0:T(128)S(1)} fusion(s32[1,32]{1,0:T(1,128)} %param.5), kind=kLoop, calls=%fused_computation.17 | loop fusion | flops 480 | bytes 256 | tf_op jit(solution)/shard_map/eq | solution.py:490
  0.7 0.0 copy-done.2
  0.7 0.7 %and_select_fusion.2 = (s32[32]{0:T(128)S(1)}, s32[32]{0:T(128)S(1)}) fusion(s32[1,32]{1,0:T(1,128)} %param.5, s32[1,3,32]{2,0,1:T(1,128)S(1)} %copy-done.2), kind=kLoop, calls=%fused_computation.7 | loop fusion | flops 800 | bytes 768 | tf_op jit(solution)/shard_map/jit(floor_divide)/jit(_where)/select_n | solution.py:488
  1.4 0.2 convert_reduce_fusion
  1.5 0.1 select_reduce_fusion
  1.6 0.1 reshape.88
  1.7 0.0 copy-start
  1.7 1.1 %copy-done = bf16[1,8,48000]{2,1,0:T(8,128)(2,1)S(1)} copy-done((bf16[1,8,48000]{2,1,0:T(8,128)(2,1)S(1)}, bf16[1,8,48000]{2,1,0:T(8,128)(2,1)}, u32[]{:S(2)}) %copy-start) | copy-done | bytes 768024
  2.9 0.0 copy-start.1
  2.9 1.0 %copy-done.1 = f32[1,3,4,64,128]{4,3,2,1,0:T(8,128)S(1)} copy-done((f32[1,3,4,64,128]{4,3,2,1,0:T(8,128)S(1)}, f32[1,3,4,64,128]{4,3,2,1,0:T(8,128)}, u32[]{:S(2)}) %copy-start.1) | copy-done | bytes 393240
  3.9 33.1 %shard_map.46 = f32[6,4,16,128]{3,2,1,0:T(8,128)S(1)} custom-call(s32[8,1,128]{2,1,0:T(1,128)S(1)} %pad.4.code_ref, s32[32]{0:T(128)S(1)} %multiply_add_fusion.slot_ref, bf16[1,8,48000]{2,1,0:T(8,128)(2,1)S(1)} %copy-done, f32[1,3,4,64,128]{4,3,2,1,0:T(8,128)S(1)} %copy-done.1), custom_call_target="tpu_custom_call" | custom-call | tf_op jit(solution)/shard_map/pallas_call | solution.py:508
  37.0 0.7 %copy.9 = f32[6,4,16,128]{3,2,1,0:T(8,128)} copy(f32[6,4,16,128]{3,2,1,0:T(8,128)S(1)} %shard_map.46) | data formatting | bytes 393216
  (2 shorter events, 0.0 us)
Async XLA Ops:
  0.0 0.7 %copy-start.2 = (s32[1,3,32]{2,0,1:T(1,128)S(1)}, s32[1,3,32]{2,0,1:T(1,128)}, u32[]{:S(2)}) copy-start(s32[1,3,32]{2,0,1:T(1,128)} %param.6) | copy-start | bytes 1156
  1.7 1.1 %copy-start = (bf16[1,8,48000]{2,1,0:T(8,128)(2,1)S(1)}, bf16[1,8,48000]{2,1,0:T(8,128)(2,1)}, u32[]{:S(2)}) copy-start(bf16[1,8,48000]{2,1,0:T(8,128)(2,1)} %brick_hbm.1) | copy-start | bytes 2304004
  2.9 1.0 %copy-start.1 = (f32[1,3,4,64,128]{4,3,2,1,0:T(8,128)S(1)}, f32[1,3,4,64,128]{4,3,2,1,0:T(8,128)}, u32[]{:S(2)}) copy-start(f32[1,3,4,64,128]{4,3,2,1,0:T(8,128)} %u_hbm.1) | copy-start | bytes 1179652

commit v5 on v4

--- a/solution.py
+++ b/solution.py
@@ -15,8 +15,9 @@
 LANES = 128
 ROWS = COMP * SLAB_Z
 BRICK_ROWS = COMP * EDGE
-PARTS = COMP // 2
-PART_ROWS = 2 * SLAB_Z
+PARTS = 1
+PART_COMP = COMP // PARTS
+PART_ROWS = PART_COMP * SLAB_Z
 SPAN = 384
 FLAT = BRICK * BRICK
 
@@ -56,7 +57,7 @@
     depth = rows.shape[0]
     layer = depth // (SLAB_Z + 2 * PAD)
     row = lax.broadcasted_iota(jnp.int32, (PART_ROWS, depth), 0)
-    offset = lax.broadcasted_iota(jnp.int32, (PART_ROWS, depth), 1) - (row // 2 * layer + row % 2)
+    offset = lax.broadcasted_iota(jnp.int32, (PART_ROWS, depth), 1) - (row // PART_COMP * layer + row % PART_COMP)
     hits, shifts = [], []
     for slot in range(capacity):
         code = codes[:, slot:slot + 1]
@@ -64,7 +65,7 @@
         hits.append(offset - jnp.broadcast_to(start, (PART_ROWS, depth)))
         shifts.append(jnp.broadcast_to(code & (LANES - 1), (PART_ROWS, LANES)))
     hit = jnp.concatenate(
-        [(hits[slot] == 2 * part).astype(jnp.float32) for part in range(PARTS) for slot in range(capacity)],
+        [(hits[slot] == PART_COMP * part).astype(jnp.float32) for part in range(PARTS) for slot in range(capacity)],
         axis=0,
     ).astype(jnp.bfloat16)
     shift = jnp.concatenate(shifts * PARTS, axis=0)
@@ -176,14 +177,18 @@
 
 
 def warp_kernel(
-    code_ref, slot_ref, brick_hbm, u_hbm, out_ref,
-    brick_ref, u_ref, asked, rows_ref, rows_half, crops, arrived, hits,
+    code_hbm, slot_hbm, brick_hbm, u_hbm, out_ref,
+    code_ref, slot_ref, brick_ref, u_ref, asked, rows_ref, rows_half, crops, arrived, hits,
     u_pad, u_rows, u_edge, u_all, u_rim, rotations, placed, fields, load_sem,
     ask_send, ask_recv, crop_send, crop_recv, u_send, u_recv, up_send, up_recv,
     down_send, down_recv, field_send, field_recv,
 ):
     count, subjects = arrived.shape[1], fields.shape[0]
     capacity = arrived.shape[2] // PART_ROWS
+    load_code = pltpu.make_async_copy(code_hbm, code_ref, load_sem.at[2])
+    load_code.start()
+    load_slot = pltpu.make_async_copy(slot_hbm, slot_ref, load_sem.at[3])
+    load_slot.start()
     load_u = pltpu.make_async_copy(u_hbm.at[0], u_ref, load_sem.at[0])
     load_u.start()
     load_bricks = pltpu.make_async_copy(brick_hbm.at[0], brick_ref, load_sem.at[1])
@@ -251,6 +256,8 @@
     neighbours = (me_k + count - 1) // count + (2 * count - 2 - me_k) // count
     pl.semaphore_wait(barrier, count - 1 + (subjects - 1) * (1 + neighbours))
 
+    load_code.wait()
+
     def ask(k):
         return remote(code_ref.at[k], asked.at[me_k], ask_send.at[k], ask_recv.at[me_k], me_s, k)
 
@@ -362,6 +369,8 @@
 
     crop(me_k, arrived)
     depth = count * capacity * PART_ROWS
+
+    load_slot.wait()
 
     def make_hits(row, carry):
         hits[row] = placing_hits(slot_ref, row, depth)
@@ -436,7 +445,7 @@
         def step(z, carry):
             rotation = [[rotations[s, z, a * 3 + b] for b in range(3)] for a in range(3)]
             tensor = [
-                fields[s, c // 2, z * 2 + c % 2].astype(jnp.float32) * (1.0 / subjects)
+                fields[s, c // PART_COMP, z * PART_COMP + c % PART_COMP].astype(jnp.float32) * (1.0 / subjects)
                 for c in range(COMP)
             ]
             rotated = reorient(tensor, rotation)
@@ -479,7 +488,6 @@
 MESH = pl.DeviceIdType.MESH
 VMEM_SPEC = pl.BlockSpec(memory_space=pltpu.VMEM)
 HBM_SPEC = pl.BlockSpec(memory_space=pltpu.HBM)
-SMEM_SPEC = pl.BlockSpec(memory_space=pltpu.SMEM)
 
 
 def slot_tables(brick_ids, brick_offsets, held, slab_count, capacity):
@@ -508,9 +516,11 @@
     return pl.pallas_call(
         warp_kernel,
         out_shape=jax.ShapeDtypeStruct((COMP, SLAB_Z, BRICK, LANES), f32),
-        in_specs=[VMEM_SPEC, SMEM_SPEC, HBM_SPEC, HBM_SPEC],
+        in_specs=[HBM_SPEC] * 4,
         out_specs=VMEM_SPEC,
         scratch_shapes=[
+            pltpu.VMEM(code.shape, jnp.int32),
+            pltpu.SMEM(slot_of.shape, jnp.int32),
             pltpu.VMEM(source_bricks.shape[1:], bf16),
             pltpu.VMEM(deformation.shape[1:], f32),
             pltpu.VMEM((slab_count, 1, LANES), jnp.int32),
@@ -527,13 +537,13 @@
             pltpu.VMEM((subjects, SLAB_Z, 9, BRICK, LANES), f32),
             pltpu.VMEM((subjects, PARTS, PART_ROWS, BRICK, LANES), bf16),
             pltpu.VMEM((subjects, PARTS, PART_ROWS, BRICK, LANES), bf16),
-            dma((2,)),
+            dma((4,)),
             per_slab, per_slab, dma((PARTS, slab_count)), dma((PARTS, slab_count)),
             per_subject, per_subject, per_subject, per_subject,
             per_subject, per_subject, dma((PARTS, subjects)), dma((PARTS, subjects)),
         ],
         compiler_params=pltpu.CompilerParams(
-            vmem_limit_bytes=48 << 20, collective_id=0, has_side_effects=True
+            vmem_limit_bytes=63 << 20, collective_id=0, has_side_effects=True
         ),
     )(code, slot_of, source_bricks, deformation)
 

time: 37.9 us -> 36.2 us (0.955)
  Pallas kernels: 33.1 us -> 31.6 us
    pallas_call x1, Pallas kernels: 33.1 us -> 31.6 us  [shards(): pl.pallas_call(warp_kernel, out_shape=jax.ShapeDtypeStruct((COMP, SLAB_Z,...]
    unnamed x7 -> x5, local copies, waits for them, and re-layouts: 2.8 us -> 2.1 us
    pad x1, local copies, waits for them, and re-layouts: 0.01 us -> 0.6 us  [shards(): jnp.pad(code.reshape(slab_count, 1, capacity), ((0, 0), (0, 0), (0, LANES...]
where the time goes in v5:
time: 36.2 us; the launch traced here: 36 us
  Pallas kernels  31.6 us (87%)
  local copies, waits for them, and re-layouts  2.78 us (8%)
  other arithmetic  1.62 us (4%)
    pallas_call x1, Pallas kernels, shards(): pl.pallas_call(warp_kernel, out_shape=jax.ShapeDtypeStruct((COMP, SLAB_Z,...  31.6 us
    unnamed x5, local copies, waits for them, and re-layouts  2.1 us

profile of v5, /device:TPU:0, one launch (start us, length us, event | category | flops | bytes accessed | tf_op | source)
XLA Modules:
  0.0 36.0 jit_solution(6643842167936876274)
XLA Ops:
  0.0 0.0 copy-start
  0.0 0.7 %fusion.2 = s32[32]{0:T(128)S(1)} fusion(s32[1,32]{1,0:T(1,128)} %param.5), kind=kLoop, calls=%fused_computation.17 | loop fusion | flops 480 | bytes 256 | tf_op jit(solution)/shard_map/eq | solution.py:498
  0.7 0.0 copy-done
  0.7 0.7 %and_select_fusion.2 = (s32[32]{0:T(128)S(1)}, s32[32]{0:T(128)S(1)}) fusion(s32[1,32]{1,0:T(1,128)} %param.5, s32[1,3,32]{2,0,1:T(1,128)S(1)} %copy-done), kind=kLoop, calls=%fused_computation.7 | loop fusion | flops 800 | bytes 768 | tf_op jit(solution)/shard_map/jit(floor_divide)/jit(_where)/select_n | solution.py:496
  1.4 0.2 convert_reduce_fusion
  1.5 0.0 copy-start.1
  1.6 0.1 select_reduce_fusion
  1.6 0.5 %copy-done.1 = s32[32]{0:T(128)} copy-done((s32[32]{0:T(128)}, s32[32]{0:T(128)S(1)}, u32[]{:S(2)}) %copy-start.1) | copy-done | bytes 152
  2.1 0.1 reshape.88
  2.2 0.6 %pad.4.code_hbm = s32[8,1,128]{2,1,0:T(1,128)} pad(s32[8,1,6]{2,1,0:T(1,128)S(1)} %bitcast.24, s32[]{:T(128)} %constant.29.clone.1), padding=0_0x0_0x0_122 | pad | bytes 4292 | tf_op jit(solution)/shard_map/jit(_pad)/pad | solution.py:513
  2.8 31.6 %shard_map.46 = f32[6,4,16,128]{3,2,1,0:T(8,128)} custom-call(s32[8,1,128]{2,1,0:T(1,128)} %pad.4.code_hbm, s32[32]{0:T(128)} %copy-done.1, bf16[1,8,48000]{2,1,0:T(8,128)(2,1)} %brick_hbm.1, f32[1,3,4,64,128]{4,3,2,1,0:T(8,128)} %u_hbm.1), custom_call_target="tpu_custom_call" | custom-call | tf_op jit(solution)/shard_map/pallas_call | solution.py:516
  34.4 1.6 %copy.9 = f32[6,4,16,128]{3,2,1,0:T(8,128)} copy(f32[6,4,16,128]{3,2,1,0:T(8,128)} %shard_map.46) | data formatting | bytes 393216
  (1 shorter events, 0.0 us)
Async XLA Ops:
  0.0 0.7 %copy-start = (s32[1,3,32]{2,0,1:T(1,128)S(1)}, s32[1,3,32]{2,0,1:T(1,128)}, u32[]{:S(2)}) copy-start(s32[1,3,32]{2,0,1:T(1,128)} %param.6) | copy-start | bytes 1156
  1.5 0.6 %copy-start.1 = (s32[32]{0:T(128)}, s32[32]{0:T(128)S(1)}, u32[]{:S(2)}) copy-start(s32[32]{0:T(128)S(1)} %multiply_add_fusion.slot_hbm) | copy-start | bytes 388

commit v6 on v4

--- a/solution.py
+++ b/solution.py
@@ -15,8 +15,9 @@
 LANES = 128
 ROWS = COMP * SLAB_Z
 BRICK_ROWS = COMP * EDGE
-PARTS = COMP // 2
-PART_ROWS = 2 * SLAB_Z
+PARTS = 1
+PART_COMP = COMP // PARTS
+PART_ROWS = PART_COMP * SLAB_Z
 SPAN = 384
 FLAT = BRICK * BRICK
 
@@ -56,7 +57,7 @@
     depth = rows.shape[0]
     layer = depth // (SLAB_Z + 2 * PAD)
     row = lax.broadcasted_iota(jnp.int32, (PART_ROWS, depth), 0)
-    offset = lax.broadcasted_iota(jnp.int32, (PART_ROWS, depth), 1) - (row // 2 * layer + row % 2)
+    offset = lax.broadcasted_iota(jnp.int32, (PART_ROWS, depth), 1) - (row // PART_COMP * layer + row % PART_COMP)
     hits, shifts = [], []
     for slot in range(capacity):
         code = codes[:, slot:slot + 1]
@@ -64,7 +65,7 @@
         hits.append(offset - jnp.broadcast_to(start, (PART_ROWS, depth)))
         shifts.append(jnp.broadcast_to(code & (LANES - 1), (PART_ROWS, LANES)))
     hit = jnp.concatenate(
-        [(hits[slot] == 2 * part).astype(jnp.float32) for part in range(PARTS) for slot in range(capacity)],
+        [(hits[slot] == PART_COMP * part).astype(jnp.float32) for part in range(PARTS) for slot in range(capacity)],
         axis=0,
     ).astype(jnp.bfloat16)
     shift = jnp.concatenate(shifts * PARTS, axis=0)
@@ -436,7 +437,7 @@
         def step(z, carry):
             rotation = [[rotations[s, z, a * 3 + b] for b in range(3)] for a in range(3)]
             tensor = [
-                fields[s, c // 2, z * 2 + c % 2].astype(jnp.float32) * (1.0 / subjects)
+                fields[s, c // PART_COMP, z * PART_COMP + c % PART_COMP].astype(jnp.float32) * (1.0 / subjects)
                 for c in range(COMP)
             ]
             rotated = reorient(tensor, rotation)

time: 37.9 us -> 36.9 us (0.974)
  Pallas kernels: 33.1 us -> 32.2 us
    pallas_call x1, Pallas kernels: 33.1 us -> 32.2 us  [shards(): pl.pallas_call(warp_kernel, out_shape=jax.ShapeDtypeStruct((COMP, SLAB_Z,...]
where the time goes in v6:
time: 36.9 us; the launch traced here: 36.7 us
  Pallas kernels  32.2 us (87%)
  local copies, waits for them, and re-layouts  2.89 us (8%)
  other arithmetic  1.63 us (4%)
    pallas_call x1, Pallas kernels, shards(): pl.pallas_call(warp_kernel, out_shape=jax.ShapeDtypeStruct((COMP, SLAB_Z,...  32.2 us
    unnamed x7, local copies, waits for them, and re-layouts  2.8 us

profile of v6, /device:TPU:0, one launch (start us, length us, event | category | flops | bytes accessed | tf_op | source)
XLA Modules:
  0.0 36.7 jit_solution(16795354654209990474)
XLA Ops:
  0.0 0.0 copy-start.2
  0.0 0.7 %fusion.2 = s32[32]{0:T(128)S(1)} fusion(s32[1,32]{1,0:T(1,128)} %param.5), kind=kLoop, calls=%fused_computation.17 | loop fusion | flops 480 | bytes 256 | tf_op jit(solution)/shard_map/eq | solution.py:491
  0.7 0.0 copy-done.2
  0.7 0.7 %and_select_fusion.2 = (s32[32]{0:T(128)S(1)}, s32[32]{0:T(128)S(1)}) fusion(s32[1,32]{1,0:T(1,128)} %param.5, s32[1,3,32]{2,0,1:T(1,128)S(1)} %copy-done.2), kind=kLoop, calls=%fused_computation.7 | loop fusion | flops 800 | bytes 768 | tf_op jit(solution)/shard_map/jit(floor_divide)/jit(_where)/select_n | solution.py:489
  1.4 0.2 convert_reduce_fusion
  1.5 0.1 select_reduce_fusion
  1.6 0.1 reshape.88
  1.7 0.0 copy-start
  1.7 1.1 %copy-done = bf16[1,8,48000]{2,1,0:T(8,128)(2,1)S(1)} copy-done((bf16[1,8,48000]{2,1,0:T(8,128)(2,1)S(1)}, bf16[1,8,48000]{2,1,0:T(8,128)(2,1)}, u32[]{:S(2)}) %copy-start) | copy-done | bytes 768024
  2.9 0.0 copy-start.1
  2.9 1.0 %copy-done.1 = f32[1,3,4,64,128]{4,3,2,1,0:T(8,128)S(1)} copy-done((f32[1,3,4,64,128]{4,3,2,1,0:T(8,128)S(1)}, f32[1,3,4,64,128]{4,3,2,1,0:T(8,128)}, u32[]{:S(2)}) %copy-start.1) | copy-done | bytes 393240
  3.9 32.2 %shard_map.46 = f32[6,4,16,128]{3,2,1,0:T(8,128)S(1)} custom-call(s32[8,1,128]{2,1,0:T(1,128)S(1)} %pad.4.code_ref, s32[32]{0:T(128)S(1)} %multiply_add_fusion.slot_ref, bf16[1,8,48000]{2,1,0:T(8,128)(2,1)S(1)} %copy-done, f32[1,3,4,64,128]{4,3,2,1,0:T(8,128)S(1)} %copy-done.1), custom_call_target="tpu_custom_call" | custom-call | tf_op jit(solution)/shard_map/pallas_call | solution.py:509
  36.0 0.7 %copy.9 = f32[6,4,16,128]{3,2,1,0:T(8,128)} copy(f32[6,4,16,128]{3,2,1,0:T(8,128)S(1)} %shard_map.46) | data formatting | bytes 393216
  (2 shorter events, 0.0 us)
Async XLA Ops:
  0.0 0.7 %copy-start.2 = (s32[1,3,32]{2,0,1:T(1,128)S(1)}, s32[1,3,32]{2,0,1:T(1,128)}, u32[]{:S(2)}) copy-start(s32[1,3,32]{2,0,1:T(1,128)} %param.6) | copy-start | bytes 1156
  1.7 1.1 %copy-start = (bf16[1,8,48000]{2,1,0:T(8,128)(2,1)S(1)}, bf16[1,8,48000]{2,1,0:T(8,128)(2,1)}, u32[]{:S(2)}) copy-start(bf16[1,8,48000]{2,1,0:T(8,128)(2,1)} %brick_hbm.1) | copy-start | bytes 2304004
  2.9 1.0 %copy-start.1 = (f32[1,3,4,64,128]{4,3,2,1,0:T(8,128)S(1)}, f32[1,3,4,64,128]{4,3,2,1,0:T(8,128)}, u32[]{:S(2)}) copy-start(f32[1,3,4,64,128]{4,3,2,1,0:T(8,128)} %u_hbm.1) | copy-start | bytes 1179652
